TPU v7x, 512 devices: a whole 4x8x8 slice. The times are simulated.
512 devices in a mesh: dp: 64 (over x, z, core), cent: 8 (over y).
Axes of the slice: x: 4, y: 8, z: 8, core: 2. Of those that a mesh axis runs over, the one named last changes fastest.
Arguments:
- vectors: bfloat16 [65536, 768], P('dp'), may hold values from -64 to 64
- centroids: bfloat16 [8192, 768], P('cent'), may hold values from -5 to 5
- prior_mass: float32 [8192], P('cent'), may hold values from 0.5 to 8
- assign: int32 [65536], P('dp'), may hold values from 0 to 8191, as said below
- owner_of: int32 [8192], replicated, may hold values from 0 to 63, as said below
- rotation: bfloat16 [768, 768], replicated, may hold values from -0.21875 to 0.21875
Outputs:
- new_centroids: float32 [8, 1024, 768], P('cent', 'dp')
- moments: float32 [64, 16, 768], P('dp', None, 'cent')
Inputs may be any that keep to these rules, and one draw needn't show every extreme that they name: `assign`: of the 1024 vectors of each dp index, exactly 128 have their list in each block of 1024 consecutive lists; of those, at most 8 have lists of one owner, and for each block of lists one owner, the same for every dp index, receives exactly 8 from every dp index. `owner_of`: each owner holds exactly 16 lists of each block of 1024 consecutive lists.
All inputs are finite; a program needn't handle non-finite values.
Results may differ from a plain program's by a relative error of at most 0.0033.
Values may be sent and summed in bfloat16 or wider, within the bound.
A program may use at most 64 MiB of HBM per device.

v0:
```python
import math

import jax
import jax.numpy as jnp
from jax import lax
from jax.sharding import Mesh
from jax.sharding import PartitionSpec as P

M = 48
DP = ("dp_0", "dp_1", "dp_2")


def copy_for_each(array, axis):
    copies = jnp.broadcast_to(array, (lax.axis_size(axis), *array.shape))
    return lax.all_to_all(copies, axis, split_axis=0, concat_axis=0, tiled=True)


def gathered_once(array, axis):
    leaves = jax.tree.leaves(array)
    sequence = sorted(range(len(leaves)), key=lambda k: -leaves[k].size)
    width = (1, *leaves[sequence[0]].shape)[-1]
    lines = [
        jnp.pad(leaves[k].reshape(-1), (0, -leaves[k].size % width)).reshape(-1, width)
        for k in sequence
    ]
    both, at, found = (copy_for_each(jnp.concatenate(lines), axis), 0, {})
    for k, line in zip(sequence, lines):
        piece = both[:, at : at + len(line)].reshape(len(both), -1)
        found[k] = piece[:, : leaves[k].size].reshape(-1, *leaves[k].shape)
        at += len(line)
    numbers = iter(range(len(leaves)))
    return jax.tree.map(lambda _: found[next(numbers)], array)


def folded_in_pairs(pieces, combine):
    while len(jax.tree.leaves(pieces)[0]) > 1:
        pieces = jax.vmap(combine)(
            *(jax.tree.map(lambda part: part[side::2], pieces) for side in (0, 1))
        )
    return jax.tree.map(lambda part: part[0], pieces)


def merged_2(array, axis, combine):
    pieces = gathered_once(array, axis)
    return folded_in_pairs(pieces, combine)


def in_blocks(array, dim, peers):
    shape = array.shape
    parts = array.reshape(*shape[:dim], peers, shape[dim] // peers, *shape[dim + 1 :])
    return jnp.moveaxis(parts, dim, 0)


def sum_at_owner(array, axis, dim):
    parts = in_blocks(array, dim, lax.axis_size(axis))
    arrived = lax.all_to_all(parts, axis, split_axis=0, concat_axis=0, tiled=True)
    return arrived.sum(axis=0)


def sum_by_axis(array, axes, dim):
    far, near = axes
    own = sum_at_owner(in_blocks(array, dim, lax.axis_size(far)), near, dim + 1)
    return jnp.sum(lax.all_to_all(own, far, 0, 0, tiled=True), axis=0)


def sent_together(arrays, axis, dim, along):
    columns = [a.reshape(*a.shape[:along], -1) for a in arrays]
    both = jnp.concatenate(columns, axis=along)
    whole, at, gathered = (sum_by_axis(both, axis, dim), 0, [])
    for a, column in zip(arrays, columns):
        piece = whole[..., at : at + column.shape[along]]
        gathered.append(piece.reshape(*piece.shape[:along], *a.shape[along:]))
        at += column.shape[along]
    return tuple(gathered)


def peak_merge(earlier, later):
    top_val = jnp.maximum(earlier[0], later[0])
    merged = earlier[1] * jnp.exp(earlier[0] - top_val) + later[1] * jnp.exp(later[0] - top_val)
    return (top_val, merged)


def body(vectors, centroids, prior_mass, assign, owner_of, rotation):
    feat_width = vectors.shape[1]
    shard_rows = centroids.shape[0]
    cent_count = lax.axis_size("cent")
    owner_count = lax.axis_size(DP)
    cent_pos = lax.axis_index("cent")
    dp_pos = lax.axis_index(DP)
    inv_root = 1.0 / math.sqrt(feat_width)
    cent_square = jnp.sum(jnp.square(centroids.astype(jnp.float32)), axis=1)
    cross_dot = lax.dot_general(
        vectors, centroids, (((1,), (1,)), ((), ())), preferred_element_type=jnp.float32
    )
    scores = (2.0 * cross_dot - cent_square[None, :]) * inv_root
    local_peak = jnp.max(scores, axis=1)
    local_exp = jnp.exp(scores - local_peak[:, None])
    peak_val, row_total = merged_2((local_peak, jnp.sum(local_exp, axis=1)), "cent", peak_merge)
    factor = jnp.exp(local_peak - peak_val) / row_total
    member_prob = (local_exp * factor[:, None]).astype(jnp.bfloat16)
    sum_rows = lax.dot_general(
        member_prob, vectors, (((0,), (0,)), ((), ())), preferred_element_type=jnp.float32
    )
    soft_mass = jnp.sum(member_prob, axis=0, dtype=jnp.float32)
    own_count = shard_rows // owner_count
    own_sums, own_mass = sent_together((sum_rows, soft_mass), (("dp_0", "dp_1"), "dp_2"), 0, 1)
    own_cent = lax.dynamic_slice_in_dim(centroids, dp_pos * own_count, own_count, 0).astype(
        jnp.float32
    )
    own_prior = lax.dynamic_slice_in_dim(prior_mass, dp_pos * own_count, own_count, 0)
    updated = (own_prior[:, None] * own_cent + own_sums) / (own_prior + own_mass)[:, None]
    row_count = assign.shape[0]
    per_shard = row_count // cent_count
    slot_cap = 4 * per_shard // owner_count
    inside = assign // shard_rows == cent_pos
    in_rank = jnp.cumsum(inside.astype(jnp.int32)) - 1
    target = jnp.where(inside, in_rank, per_shard)
    picked = (
        jnp.zeros((per_shard,), jnp.int32)
        .at[target]
        .set(jnp.arange(row_count, dtype=jnp.int32), mode="drop")
    )
    list_ids = assign[picked]
    owners = owner_of[list_ids]
    local_list = list_ids - cent_pos * shard_rows
    residual = (
        vectors[picked].astype(jnp.float32) - centroids[local_list].astype(jnp.float32)
    ).astype(jnp.bfloat16)
    member = (owners[:, None] == jnp.arange(owner_count, dtype=jnp.int32)[None, :]).astype(
        jnp.int32
    )
    in_order = jnp.sum(jnp.cumsum(member, axis=0) * member, axis=1) - 1
    slot_ids = owners * slot_cap + in_order
    empty_rows = jnp.zeros((owner_count * slot_cap, feat_width), jnp.bfloat16)
    turned_rows = jnp.dot(residual, rotation, preferred_element_type=jnp.float32).astype(
        jnp.bfloat16
    )
    packed = empty_rows.at[slot_ids].set(turned_rows).reshape(owner_count, slot_cap, feat_width)
    rotated = lax.all_to_all(packed, DP, split_axis=0, concat_axis=0, tiled=True)
    sub_width = feat_width // M
    flat_rows = rotated.reshape(owner_count * slot_cap, M, sub_width)
    per_space = jnp.transpose(flat_rows, (1, 0, 2))
    local_moments = lax.dot_general(
        per_space, per_space, (((1,), (1,)), ((0,), (0,))), preferred_element_type=jnp.float32
    )
    local_moments = jnp.transpose(local_moments, (1, 0, 2)).reshape(sub_width, feat_width)
    moment_part = sum_at_owner(local_moments, "cent", 1)
    moment_part = moment_part / vectors.shape[0]
    return (updated[None], moment_part[None])


def solution(mesh):
    finer = Mesh(
        mesh.devices.reshape(4, 8, 2, mesh.shape["cent"]), ("dp_0", "dp_1", "dp_2", "cent")
    )
    in_specs = (P(DP, None), P("cent", None), P("cent"), P(DP), P(), P())
    out_specs = (P("cent", DP, None), P(DP, None, "cent"))
    return jax.shard_map(body, mesh=finer, in_specs=in_specs, out_specs=out_specs, check_vma=False)
```

profile of v0, /device:TPU:1, one launch (start us, length us, event | category | flops | bytes accessed | tf_op | source)
XLA Modules:
  0.0 153.5 jit_solution(5234296496366153180)
XLA Ops:
  0.6 1.9 %multiply_reduce_fusion = f32[1024]{0:T(1024)S(1)} fusion(bf16[1024,768]{1,0:T(8,128)(2,1)} %param.7), kind=kLoop, calls=%fused_computation.12 | loop fusion | flops 2358272 | bytes 1576960 | tf_op jit(solution)/shard_map/reduce_sum | solution.py:91
  2.6 3.2 %fusion.1 = (f32[1024]{0:T(1024)S(1)}, f32[1024,1024]{0,1:T(8,128)S(1)}) fusion(f32[1024]{0:T(1024)S(1)} %multiply_reduce_fusion, bf16[1024,768]{1,0:T(8,128)(2,1)S(1)} %copy-done, bf16[1024,768]{1,0:T(8,128)(2,1)} %param.7), kind=kOutput, calls=%fused_computation.13 | convolution fusion | flops 1614806016 | bytes 7348224 | tf_op jit(solution)/shard_map/dot_general | solution.py:92
  5.8 1.9 %copy-done.2 = f32[1024,1024]{0,1:T(8,128)} copy-done((f32[1024,1024]{0,1:T(8,128)}, f32[1024,1024]{0,1:T(8,128)S(1)}, u32[]{:S(2)}) %copy-start.2) | copy-done | bytes 4194328
  7.7 1.0 fusion
  9.4 7.6 %all-to-all-start = ((f32[8,2,1024]{2,1,0:T(2,128)}), f32[8,2,1024]{2,1,0:T(2,128)S(1)}, u32[]{:S(2)}, u32[]{:S(2)}) async-start(f32[8,2,1024]{2,1,0:T(2,128)} %broadcast_in_dim.14), calls=%async_computation | async-start | bytes 131072 | tf_op jit(solution)/shard_map/all_to_all | solution.py:15
  17.7 4.3 %scatter_custom_fusion = s32[128]{0:T(128)S(1)} fusion(s32[1024]{0:T(1024)S(1)} %compare_select_fusion, s32[1024]{0:T(1024)S(1)} %iota.7, s32[]{:T(128)} %constant.32.clone.1), kind=kCustom, calls=%fused_computation.61 | custom fusion | bytes 516 | tf_op jit(solution)/shard_map/scatter | solution.py:121
  23.9 1.1 gather_fusion.1
  27.0 1.5 %gather_fusion.3 = bf16[128,768]{1,0:T(8,128)(2,1)} fusion(bf16[1024,768]{1,0:T(8,128)(2,1)S(1)} %copy-done.4, s32[1024]{0:T(1024)S(1)} %get-tuple-element.22), kind=kCustom, calls=%fused_computation.3 | custom fusion | bytes 393728 | tf_op jit(solution)/shard_map/gather | solution.py:127
  28.5 1.7 %convolution_convert_fusion = bf16[128,768]{1,0:T(8,128)(2,1)S(1)} fusion(bf16[768,768]{1,0:T(8,128)(2,1)} %param.11, bf16[128,768]{1,0:T(8,128)(2,1)} %gather_fusion.3, bf16[128,768]{1,0:T(8,128)(2,1)S(1)} %gather_fusion.2), kind=kOutput, calls=%fused_computation.15 | convolution fusion | flops 151486464 | bytes 1769472 | tf_op jit(solution)/shard_map/dot_general | solution.py:135
  30.2 2.1 %scatter_custom_fusion.1 = bf16[512,768]{1,0:T(8,128)(2,1)} fusion(s32[128]{0:T(128)S(1)} %fusion.13, bf16[128,768]{1,0:T(8,128)(2,1)S(1)} %convolution_convert_fusion, bf16[]{:T(256)} %constant.65.clone.1), kind=kCustom, calls=%fused_computation.18 | custom fusion | bytes 786434 | tf_op jit(solution)/shard_map/scatter | solution.py:138
  32.3 14.3 %all-to-all-start.3 = ((bf16[64,8,768]{2,1,0:T(8,128)(2,1)}), bf16[64,8,768]{2,1,0:T(8,128)(2,1)S(1)}, u32[]{:S(2)}, u32[]{:S(2)}) async-start(bf16[64,8,768]{2,1,0:T(8,128)(2,1)} %bitcast.15), calls=%async_computation.3 | async-start | bytes 1572864 | tf_op jit(solution)/shard_map/all_to_all | solution.py:139
  47.0 4.9 %convert_reduce_fusion = (f32[1024]{0:T(1024)S(1)}, bf16[1024,1024]{0,1:T(8,128)(2,1)}) fusion(f32[1024]{0:T(1024)S(1)} %exponential_divide_fusion, f32[1024]{0:T(1024)S(1)} %get-tuple-element.18, f32[1024]{0:T(1024)S(1)} %multiply_reduce_fusion, f32[1024,1024]{0,1:T(8,128)} %copy-done.2), kind=kLoop, calls=%fused_computation.6 | loop fusion | flops 8387584 | bytes 6307840 | tf_op jit(solution)/shard_map/reduce_sum | solution.py:104
  52.4 3.4 %fusion.20 = f32[1024,768]{1,0:T(8,128)S(1)} fusion(bf16[1024,1024]{0,1:T(8,128)(2,1)} %get-tuple-element.7, bf16[1024,768]{1,0:T(8,128)(2,1)S(1)} %copy-done), kind=kOutput, calls=%fused_computation.65 | convolution fusion | flops 1610612736 | bytes 6815744 | tf_op jit(solution)/shard_map/dot_general | solution.py:101
  55.8 2.2 %maximum_bitcast_fusion = f32[2,32,16,769]{3,2,1,0:T(8,128)} fusion(f32[32,2,16,1]{3,2,0,1:T(8,128)S(1)} %copy.21, f32[32,2,16,768]{3,2,1,0:T(8,128)S(1)} %bitcast.46), kind=kLoop, calls=%fused_computation.11 | loop fusion | flops 787456 | bytes 6299648 | tf_op jit(solution)/shard_map/transpose | solution.py:51
  58.0 11.5 %all-to-all-done.3 = bf16[64,8,768]{2,1,0:T(8,128)(2,1)S(1)} async-done(((bf16[64,8,768]{2,1,0:T(8,128)(2,1)}), bf16[64,8,768]{2,1,0:T(8,128)(2,1)S(1)}, u32[]{:S(2)}, u32[]{:S(2)}) %all-to-all-start.3) | async-done | bytes 786464 | tf_op jit(solution)/shard_map/all_to_all | solution.py:139
  69.6 5.8 %all-to-all-start.1 = ((f32[2,32,16,769]{3,2,1,0:T(8,128)}), f32[2,32,16,769]{3,2,1,0:T(8,128)}, u32[]{:S(2)}, u32[]{:S(2)}) async-start(f32[2,32,16,769]{3,2,1,0:T(8,128)} %maximum_bitcast_fusion), calls=%async_computation.1 | async-start | bytes 7340032 | tf_op jit(solution)/shard_map/all_to_all | solution.py:56
  75.3 5.9 %reshape.141 = bf16[512,48,16]{2,1,0:T(8,128)(2,1)} reshape(bf16[64,8,768]{2,1,0:T(8,128)(2,1)S(1)} %all-to-all-done.3) | data formatting | bytes 1572864 | tf_op jit(solution)/shard_map/reshape | solution.py:141
  81.2 6.3 %copy.22 = bf16[512,48,16]{0,2,1:T(8,128)(2,1)S(1)} copy(bf16[512,48,16]{2,1,0:T(8,128)(2,1)} %reshape.141) | data formatting | bytes 1572864 | tf_op jit(solution)/shard_map/reshape | solution.py:141
  88.9 6.9 %all-to-all-start.4 = ((f32[8,16,96]{2,1,0:T(8,128)}), f32[8,16,96]{2,1,0:T(8,128)S(1)}, u32[]{:S(2)}, u32[]{:S(2)}) async-start(f32[8,16,96]{2,1,0:T(8,128)} %copy.24), calls=%async_computation.4 | async-start | bytes 131072 | tf_op jit(solution)/shard_map/all_to_all | solution.py:56
  95.8 3.8 %reduce_sum.66 = f32[32,16,769]{2,1,0:T(8,128)} reduce(f32[2,32,16,769]{3,2,1,0:T(8,128)} %all-to-all-done.1, f32[]{:T(128)} %constant.62.clone.1), dimensions={0}, to_apply=%region_4.5 | reduce | flops 393728 | bytes 4724740 | tf_op jit(solution)/shard_map/reduce_sum | solution.py:57
  99.6 3.4 %all-to-all-done.4 = f32[8,16,96]{2,1,0:T(8,128)S(1)} async-done(((f32[8,16,96]{2,1,0:T(8,128)}), f32[8,16,96]{2,1,0:T(8,128)S(1)}, u32[]{:S(2)}, u32[]{:S(2)}) %all-to-all-start.4) | async-done | bytes 49184 | tf_op jit(solution)/shard_map/all_to_all | solution.py:56
  103.0 5.4 %all-to-all-start.2 = ((f32[32,16,769]{2,1,0:T(8,128)}), f32[32,16,769]{2,1,0:T(8,128)S(1)}, u32[]{:S(2)}, u32[]{:S(2)}) async-start(f32[32,16,769]{2,1,0:T(8,128)} %reduce_sum.66), calls=%async_computation.2 | async-start | bytes 3670016 | tf_op jit(solution)/shard_map/all_to_all | solution.py:63
  109.0 42.0 %all-to-all-done.2 = f32[32,16,769]{2,1,0:T(8,128)S(1)} async-done(((f32[32,16,769]{2,1,0:T(8,128)}), f32[32,16,769]{2,1,0:T(8,128)S(1)}, u32[]{:S(2)}, u32[]{:S(2)}) %all-to-all-start.2) | async-done | bytes 1574944 | tf_op jit(solution)/shard_map/all_to_all | solution.py:63
  152.1 1.4 fusion.7
  (55 shorter events, 8.8 us)
Async XLA Ops:
  0.6 1.9 %copy-start = (bf16[1024,768]{1,0:T(8,128)(2,1)S(1)}, bf16[1024,768]{1,0:T(8,128)(2,1)}, u32[]{:S(2)}) copy-start(bf16[1024,768]{1,0:T(8,128)(2,1)} %param.6) | copy-start | bytes 4718596
  5.8 1.9 %copy-start.2 = (f32[1024,1024]{0,1:T(8,128)}, f32[1024,1024]{0,1:T(8,128)S(1)}, u32[]{:S(2)}) copy-start(f32[1024,1024]{0,1:T(8,128)S(1)} %get-tuple-element.19) | copy-start | bytes 12582916
  5.8 11.2 %copy-start.1 = (s32[1024]{0:T(1024)S(1)}, s32[1024]{0:T(1024)}, u32[]{:S(2)}) copy-start(s32[1024]{0:T(1024)} %param.9) | copy-start | bytes 12292
  5.8 18.1 %copy-start.3 = (s32[8192]{0:T(1024)S(1)}, s32[8192]{0:T(1024)}, u32[]{:S(2)}) copy-start(s32[8192]{0:T(1024)} %param.10) | copy-start | bytes 98308
  7.7 19.2 %copy-start.4 = (bf16[1024,768]{1,0:T(8,128)(2,1)S(1)}, bf16[1024,768]{1,0:T(8,128)(2,1)}, u32[]{:S(2)}) copy-start(bf16[1024,768]{1,0:T(8,128)(2,1)} %param.7) | copy-start | bytes 4718596
  9.4 22.9 %all-to-all-start = ((f32[8,2,1024]{2,1,0:T(2,128)}), f32[8,2,1024]{2,1,0:T(2,128)S(1)}, u32[]{:S(2)}, u32[]{:S(2)}) async-start(f32[8,2,1024]{2,1,0:T(2,128)} %broadcast_in_dim.14), calls=%async_computation | async-start | bytes 131072 | tf_op jit(solution)/shard_map/all_to_all | solution.py:15
  32.3 37.2 %all-to-all-start.3 = ((bf16[64,8,768]{2,1,0:T(8,128)(2,1)}), bf16[64,8,768]{2,1,0:T(8,128)(2,1)S(1)}, u32[]{:S(2)}, u32[]{:S(2)}) async-start(bf16[64,8,768]{2,1,0:T(8,128)(2,1)} %bitcast.15), calls=%async_computation.3 | async-start | bytes 1572864 | tf_op jit(solution)/shard_map/all_to_all | solution.py:139
  69.6 19.3 %all-to-all-start.1 = ((f32[2,32,16,769]{3,2,1,0:T(8,128)}), f32[2,32,16,769]{3,2,1,0:T(8,128)}, u32[]{:S(2)}, u32[]{:S(2)}) async-start(f32[2,32,16,769]{3,2,1,0:T(8,128)} %maximum_bitcast_fusion), calls=%async_computation.1 | async-start | bytes 7340032 | tf_op jit(solution)/shard_map/all_to_all | solution.py:56
  88.9 14.1 %all-to-all-start.4 = ((f32[8,16,96]{2,1,0:T(8,128)}), f32[8,16,96]{2,1,0:T(8,128)S(1)}, u32[]{:S(2)}, u32[]{:S(2)}) async-start(f32[8,16,96]{2,1,0:T(8,128)} %copy.24), calls=%async_computation.4 | async-start | bytes 131072 | tf_op jit(solution)/shard_map/all_to_all | solution.py:56
  103.0 48.1 %all-to-all-start.2 = ((f32[32,16,769]{2,1,0:T(8,128)}), f32[32,16,769]{2,1,0:T(8,128)S(1)}, u32[]{:S(2)}, u32[]{:S(2)}) async-start(f32[32,16,769]{2,1,0:T(8,128)} %reduce_sum.66), calls=%async_computation.2 | async-start | bytes 3670016 | tf_op jit(solution)/shard_map/all_to_all | solution.py:63
where the time goes:
time: 156 us; the launch traced here: 154 us
  waiting for transfers between devices  57 us (37%)
  starting transfers between devices  40 us (26%)
  local copies, waits for them, and re-layouts  27.8 us (18%)
  other arithmetic  19.1 us (12%)
  matrix products  8.69 us (6%)
    all_to_all x1, waiting for transfers between devices, sum_by_axis(): return jnp.sum(lax.all_to_all(own, far, 0, 0, tiled=True), axis=0)  42 us
    all_to_all x1, starting transfers between devices, body(): lax.all_to_all(packed, DP, split_axis=0, concat_axis=0, tiled=True)  14.3 us
    all_to_all x2, starting transfers between devices, sum_at_owner(): lax.all_to_all(parts, axis, split_axis=0, concat_axis=0, tiled=True)  12.7 us
    reshape x2, local copies, waits for them, and re-layouts, body(): flat_rows = rotated.reshape(owner_count * slot_cap, M, sub_width)  12.3 us
    all_to_all x1, waiting for transfers between devices, body(): lax.all_to_all(packed, DP, split_axis=0, concat_axis=0, tiled=True)  11.5 us
    all_to_all x1, starting transfers between devices, copy_for_each(): return lax.all_to_all(copies, axis, split_axis=0, concat_axis=0, tiled=True)  7.64 us
    all_to_all x1, starting transfers between devices, sum_by_axis(): return jnp.sum(lax.all_to_all(own, far, 0, 0, tiled=True), axis=0)  5.38 us
    reduce_sum x1, other arithmetic, body(): soft_mass = jnp.sum(member_prob, axis=0, dtype=jnp.float32)  4.87 us
  transfers between devices with their start and end apart: 5, of which 3 were waited for; matrix products, arithmetic and copies ran while one was open for 29% of the time, Pallas kernels for 0%

commit v1 on v0

v1 whole, which is shorter than its diff:
```python
import functools
import math

import jax
import jax.numpy as jnp
from jax import lax
from jax.experimental import pallas as pl
from jax.experimental.pallas import tpu as pltpu
from jax.sharding import Mesh
from jax.sharding import PartitionSpec as P

F32 = jnp.float32
BF16 = jnp.bfloat16
DP = ("dp_0", "dp_1", "dp_2")
NX, NZ, NC, NY = 4, 8, 2, 8
OWN = 16
SUBS = 48
WIDTHS = (256, 256, 256, 128)


def dot(a, b, dims=((1,), (0,))):
    return lax.dot_general(a, b, (dims, ((), ())), preferred_element_type=F32)


def kernel(
    vec_hbm, cent_hbm, rot_hbm, assign_ref, owner_ref, out_ref,
    vec, cent, rot, score, prob, extra, stat_out, stat_in, rows_out, rows_in,
    own0, own1, own2, own3, snd0, snd1, snd2, snd3, rcv0, rcv1, rcv2, rcv3,
    xs0, xs1, xs2, xs3, xr0, xr1, xr2, xr3,
    zs0, zs1, zs2, zs3, zr0, zr1, zr2, zr3,
    load_sem, stat_ss, stat_rs, rows_ss, rows_rs, core_ss, core_rs, x_ss, x_rs, z_ss, z_rs,
):
    own, snd, rcv = (own0, own1, own2, own3), (snd0, snd1, snd2, snd3), (rcv0, rcv1, rcv2, rcv3)
    xs, xr = (xs0, xs1, xs2, xs3), (xr0, xr1, xr2, xr3)
    zs, zr = (zs0, zs1, zs2, zs3), (zr0, zr1, zr2, zr3)
    px, pz, pc = (lax.axis_index(name) for name in DP)
    py = lax.axis_index("cent")
    rows, width = vec.shape
    per_shard = rows // NY
    inv_root = 1.0 / math.sqrt(width)

    loads = [
        pltpu.make_async_copy(src, dst, load_sem.at[k])
        for k, (src, dst) in enumerate(((vec_hbm, vec), (cent_hbm, cent), (rot_hbm, rot)))
    ]
    for load in loads:
        load.start()

    barrier = pltpu.get_barrier_semaphore()
    partners = [{"cent": lax.rem(py + j, NY)} for j in range(1, NY)]
    partners += [{"dp_2": lax.rem(pc + 1, NC)}]
    partners += [{"dp_0": lax.rem(px + j, NX)} for j in (1, NX - 1)]
    partners += [{"dp_1": lax.rem(pz + j, NZ)} for j in (1, NZ - 1)]
    for partner in partners:
        pl.semaphore_signal(
            barrier, inc=1, device_id=partner, device_id_type=pl.DeviceIdType.MESH
        )

    def remote(src, dst, ss, rs, device):
        return pltpu.make_async_remote_copy(
            src_ref=src, dst_ref=dst, send_sem=ss, recv_sem=rs,
            device_id=device, device_id_type=pl.DeviceIdType.MESH,
        )

    loads[0].wait()
    loads[1].wait()

    tile = 256

    def score_tile(t, top):
        rc = t // 2
        blocks = []
        for step in range(2):
            rx = lax.rem(t, 2) * 2 + step
            for rz in range(NZ):
                blocks.append(
                    cent[lax.rem(px + rx, NX), lax.rem(pz + rz, NZ), lax.rem(pc + rc, NC)]
                )
        lhs = jnp.concatenate(blocks, axis=0)
        wide = lhs.astype(F32)
        square = jnp.sum(wide * wide, axis=1, keepdims=True)
        got = (2.0 * dot(lhs, vec[...], ((1,), (1,))) - square) * inv_root
        score[pl.ds(pl.multiple_of(t * tile, tile), tile), :] = got
        return jnp.maximum(top, jnp.max(got.reshape(tile // 8, 8, rows), axis=0))

    top = lax.fori_loop(0, 4, score_tile, jnp.full((8, rows), -jnp.inf, F32))
    top = jnp.max(top, axis=0, keepdims=True)

    def exp_tile(t, total):
        at = pl.ds(pl.multiple_of(t * 128, 128), 128)
        got = jnp.exp(score[at, :] - top)
        score[at, :] = got
        return total + jnp.sum(got.reshape(16, 8, rows), axis=0)

    total = lax.fori_loop(0, 8, exp_tile, jnp.zeros((8, rows), F32))
    total = jnp.sum(total, axis=0, keepdims=True)
    for j in range(8):
        stat_out[j : j + 1, :] = top[:, 128 * j : 128 * (j + 1)]
        stat_out[8 + j : 9 + j, :] = total[:, 128 * j : 128 * (j + 1)]

    pl.semaphore_wait(barrier, len(partners))
    stat_copies = [
        remote(stat_out, stat_in.at[j - 1], stat_ss.at[j - 1], stat_rs.at[j - 1],
               {"cent": lax.rem(py + j, NY)})
        for j in range(1, NY)
    ]
    for copy in stat_copies:
        copy.start()

    lists = assign_ref[...]
    inside = lax.shift_right_logical(lists, 10) == py
    flag = inside.astype(F32).astype(BF16)
    lane_r = lax.broadcasted_iota(jnp.int32, (128, 128), 0)
    lane_c = lax.broadcasted_iota(jnp.int32, (128, 128), 1)
    before = dot(flag, (lane_r < lane_c).astype(F32).astype(BF16))
    whole = dot(flag, jnp.ones((128, 128), BF16)).astype(BF16)
    sub_r = lax.broadcasted_iota(jnp.int32, (8, 8), 0)
    sub_c = lax.broadcasted_iota(jnp.int32, (8, 8), 1)
    earlier = dot((sub_c < sub_r).astype(F32).astype(BF16), whole)
    rank = jnp.where(inside, before + earlier, -1.0)
    local = jnp.bitwise_and(lists, 1023).astype(F32)
    holder = owner_ref[py].astype(F32)

    def as_row(a):
        return jnp.concatenate([a[j : j + 1, :] for j in range(8)], axis=1)

    slot = lax.broadcasted_iota(jnp.int32, (per_shard, rows), 0).astype(F32)
    place = lax.broadcasted_iota(jnp.int32, (per_shard, rows), 1).astype(F32)
    pick = slot == as_row(rank)
    list_of = jnp.sum(jnp.where(pick, as_row(local), 0.0), axis=1, keepdims=True)
    member = place == list_of
    owner_col = jnp.sum(jnp.where(member, as_row(holder), 0.0), axis=1, keepdims=True)
    vec_rows = dot(pick.astype(F32).astype(BF16), vec[...])
    cent_rows = dot(member.astype(F32).astype(BF16), cent[...].reshape(rows, width))
    residual = (vec_rows - cent_rows).astype(BF16)
    loads[2].wait()
    turned = dot(residual, rot[...])
    span = width // NY
    pad = jnp.broadcast_to(owner_col, (per_shard, 128 - span))
    for c in range(NY):
        rows_out[c] = jnp.concatenate(
            [turned[:, span * c : span * (c + 1)], pad], axis=1
        ).astype(BF16)
    row_copies = [
        remote(rows_out.at[lax.rem(py + j, NY)], rows_in.at[j - 1],
               rows_ss.at[j - 1], rows_rs.at[j - 1], {"cent": lax.rem(py + j, NY)})
        for j in range(1, NY)
    ]
    for copy in row_copies:
        copy.start()

    for copy in stat_copies:
        copy.wait_recv()
    own_top, own_total = stat_out[0:8, :], stat_out[8:16, :]
    peak = own_top
    for j in range(NY - 1):
        peak = jnp.maximum(peak, stat_in[j, 0:8, :])
    scale = jnp.exp(own_top - peak)
    whole_total = own_total * scale
    for j in range(NY - 1):
        whole_total += stat_in[j, 8:16, :] * jnp.exp(stat_in[j, 0:8, :] - peak)
    factor = as_row(scale / whole_total)

    def prob_tile(t, carry):
        at = pl.ds(pl.multiple_of(t * 128, 128), 128)
        got = (score[at, :] * factor).astype(BF16)
        prob[at, :] = got
        mass = jnp.sum(got.astype(F32), axis=1, keepdims=True)
        high = mass.astype(BF16).astype(F32)
        lane = lax.broadcasted_iota(jnp.int32, (128, 128), 1)
        extra[at, :] = jnp.where(lane == 96, high, jnp.where(lane == 97, mass - high, 0.0))
        return carry

    lax.fori_loop(0, 8, prob_tile, 0)

    half = rows // 2
    sibling = {"dp_2": lax.rem(pc + 1, NC)}
    x_up, x_down = {"dp_0": lax.rem(px + 1, NX)}, {"dp_0": lax.rem(px + NX - 1, NX)}
    z_up, z_down = {"dp_1": lax.rem(pz + 1, NZ)}, {"dp_1": lax.rem(pz + NZ - 1, NZ)}
    core_copies = [
        remote(snd[c], rcv[c], core_ss.at[c], core_rs.at[c], sibling) for c in range(4)
    ]

    def x_copy(c, step, side):
        size = 64 if step == 0 else 128
        k = (c * 2 + step) * 2 + side
        at = pl.ds(0 if step == 0 else 64, size)
        return remote(xs[c].at[side, at], xr[c].at[side, at], x_ss.at[k], x_rs.at[k],
                      (x_up, x_down)[side])

    def z_copy(c, step, side):
        k = (c * 4 + step) * 2 + side
        size = 8 if step == 0 else 16
        at = pl.ds(0, size)
        return remote(zs[c].at[step, side, at], zr[c].at[step, side, at],
                      z_ss.at[k], z_rs.at[k], (z_up, z_down)[side])

    def stage_a(c):
        columns = vec[:, 256 * c : 256 * (c + 1)]
        snd[c][...] = dot(prob[half:, :], columns).astype(BF16)
        core_copies[c].start()
        own[c][...] = dot(prob[:half, :], columns)

    def stage_moments():
        for copy in row_copies:
            copy.wait_recv()
        got = jnp.concatenate([rows_out[py]] + [rows_in[j] for j in range(NY - 1)], axis=0)
        mine = got[:, 96:97].astype(F32)
        q = lax.broadcasted_iota(jnp.int32, (rows, 64), 1)
        qc, qx, qz = q // 32, (q // 8) % 4, q % 8
        wanted = (((px + qx) % NX) * NZ + (pz + qz) % NZ) * NC + (pc + qc) % NC
        chosen = (wanted.astype(F32) == mine).astype(F32).astype(BF16)
        from_lane = lax.broadcasted_iota(jnp.int32, (128, 256), 0)
        to_lane = lax.broadcasted_iota(jnp.int32, (128, 256), 1)
        twice = got.astype(F32)
        twice = jnp.concatenate([twice, twice], axis=1)
        ones = jnp.ones((1, 1), F32)
        keep = lax.broadcasted_iota(jnp.int32, (64, 128), 1) < 96
        for pair in range(8):
            source = (to_lane % 128) // 16 * 16 + 2 * pair + to_lane // 128
            spread = dot(got, (from_lane == source).astype(F32).astype(BF16))
            both = dot(chosen, (spread * twice).astype(BF16), ((0,), (0,)))
            for side in range(2):
                part = jnp.where(keep, both[:, 128 * side : 128 * (side + 1)], 0.0)
                a = 2 * pair + side
                moment = extra.reshape(64, OWN, 128)
                moment[:, a, :] = moment[:, a, :] + part
        snd[3][...] = extra[half:, :].astype(BF16)
        core_copies[3].start()
        own[3][...] = extra[:half, :]

    def stage_b(c):
        core_copies[c].wait_recv()
        far = own[c][256:384, :] + rcv[c][256:384, :].astype(F32)
        xs[c][0, 0:64] = far[0:64].astype(BF16)
        xs[c][1, 0:64] = far[64:128].astype(BF16)
        for side in range(2):
            x_copy(c, 0, side).start()
        for at in (slice(0, 256), slice(384, 512)):
            own[c][at, :] = own[c][at, :] + rcv[c][at, :].astype(F32)

    def stage_c(c):
        for side in range(2):
            x_copy(c, 0, side).wait_recv()
        xs[c][0, 64:128] = (own[c][128:192, :] + xr[c][0, 0:64].astype(F32)).astype(BF16)
        xs[c][0, 128:192] = own[c][192:256, :].astype(BF16)
        xs[c][1, 64:128] = own[c][384:448, :].astype(BF16)
        xs[c][1, 128:192] = (own[c][448:512, :] + xr[c][1, 0:64].astype(F32)).astype(BF16)
        for side in range(2):
            x_copy(c, 1, side).start()

    def stage_d(c):
        for side in range(2):
            x_copy(c, 1, side).wait_recv()
        own[c][0:128, :] = (
            own[c][0:128, :]
            + xr[c][0, 64:192].astype(F32)
            + xr[c][1, 64:192].astype(F32)
        )
        zs[c][0, 0, 0:8] = own[c][64:72, :]
        zs[c][0, 1, 0:8] = own[c][72:80, :]
        for side in range(2):
            z_copy(c, 0, side).start()

    def stage_z(c, step):
        for side in range(2):
            z_copy(c, step - 1, side).wait_recv()
        up, down = 16 * (4 - step), 16 * (4 + step)
        if step == 1:
            zs[c][1, 0, 0:8] = own[c][up : up + 8, :] + zr[c][0, 0, 0:8]
            zs[c][1, 0, 8:16] = own[c][up + 8 : up + 16, :]
            zs[c][1, 1, 0:8] = own[c][down : down + 8, :]
            zs[c][1, 1, 8:16] = own[c][down + 8 : down + 16, :] + zr[c][0, 1, 0:8]
        else:
            zs[c][step, 0] = own[c][up : up + 16, :] + zr[c][step - 1, 0]
            zs[c][step, 1] = own[c][down : down + 16, :] + zr[c][step - 1, 1]
        for side in range(2):
            z_copy(c, step, side).start()

    def stage_end(c):
        for side in range(2):
            z_copy(c, 3, side).wait_recv()
        at = 256 * c
        out_ref[:, at : at + WIDTHS[c]] = own[c][0:16, :] + zr[c][3, 0] + zr[c][3, 1]

    stages = [
        lambda c: stage_a(c) if c < 3 else stage_moments(),
        stage_b, stage_c, stage_d,
        lambda c: stage_z(c, 1), lambda c: stage_z(c, 2), lambda c: stage_z(c, 3),
        stage_end,
    ]
    for wave in range(len(stages) + 3):
        for c in range(4):
            if 0 <= wave - c < len(stages):
                stages[wave - c](c)

    for copy in stat_copies + row_copies + core_copies:
        copy.wait_send()
    for c in range(4):
        for side in range(2):
            for step in range(2):
                x_copy(c, step, side).wait_send()
            for step in range(4):
                z_copy(c, step, side).wait_send()


def body(vectors, centroids, prior_mass, assign, owner_of, rotation):
    rows, width = vectors.shape
    dp_pos = lax.axis_index(DP)
    own_count = centroids.shape[0] // (NX * NZ * NC)
    half = rows // 2
    any_spec = pl.BlockSpec(memory_space=pl.ANY)
    vmem_spec = pl.BlockSpec(memory_space=pltpu.VMEM)
    dma = pltpu.SemaphoreType.DMA
    scratch = [
        pltpu.VMEM((rows, width), BF16),
        pltpu.VMEM((NX, NZ, NC, OWN, width), BF16),
        pltpu.VMEM((width, width), BF16),
        pltpu.VMEM((rows, rows), F32),
        pltpu.VMEM((rows, rows), BF16),
        pltpu.VMEM((rows, 128), F32),
        pltpu.VMEM((16, 128), F32),
        pltpu.VMEM((NY - 1, 16, 128), F32),
        pltpu.VMEM((NY, 128, 128), BF16),
        pltpu.VMEM((NY - 1, 128, 128), BF16),
    ]
    scratch += [pltpu.VMEM((half, w), F32) for w in WIDTHS]
    scratch += [pltpu.VMEM((half, w), BF16) for w in WIDTHS] * 2
    scratch += [pltpu.VMEM((2, 192, w), BF16) for w in WIDTHS] * 2
    scratch += [pltpu.VMEM((4, 2, 16, w), F32) for w in WIDTHS] * 2
    scratch += [dma((3,))] + [dma((7,))] * 4 + [dma((4,))] * 2 + [dma((16,))] * 2 + [dma((32,))] * 2
    got = pl.pallas_call(
        kernel,
        out_shape=jax.ShapeDtypeStruct((OWN, sum(WIDTHS)), F32),
        in_specs=[any_spec] * 3 + [vmem_spec] * 2,
        out_specs=vmem_spec,
        scratch_shapes=scratch,
        compiler_params=pltpu.CompilerParams(
            collective_id=0, has_side_effects=True, vmem_limit_bytes=48 * 1024 * 1024
        ),
    )(
        vectors,
        centroids.reshape(NX, NZ, NC, OWN, width),
        rotation,
        assign.reshape(8, 128),
        owner_of.reshape(NY, 8, 128),
    )
    own_sums = got[:, :width]
    own_mass = got[:, width + 96] + got[:, width + 97]
    own_cent = lax.dynamic_slice_in_dim(centroids, dp_pos * own_count, own_count, 0).astype(F32)
    own_prior = lax.dynamic_slice_in_dim(prior_mass, dp_pos * own_count, own_count, 0)
    updated = (own_prior[:, None] * own_cent + own_sums) / (own_prior + own_mass)[:, None]
    moments = got[:, width : width + 96] / rows
    return (updated[None], moments[None])


def solution(mesh):
    finer = Mesh(
        mesh.devices.reshape(NX, NZ, NC, mesh.shape["cent"]), ("dp_0", "dp_1", "dp_2", "cent")
    )
    in_specs = (P(DP, None), P("cent", None), P("cent"), P(DP), P(), P())
    out_specs = (P("cent", DP, None), P(DP, None, "cent"))
    return jax.shard_map(body, mesh=finer, in_specs=in_specs, out_specs=out_specs, check_vma=False)
```

time: 156 us -> 65.5 us (0.42)
  the two profiles are of different devices: /device:TPU:1 before, /device:TPU:6 now
where the time goes in v1:
time: 65.5 us; the launch traced here: 65.2 us
  Pallas kernels  56.7 us (87%)
  local copies, waits for them, and re-layouts  5.52 us (8%)
  other arithmetic  2.25 us (3%)
  between operations  0.66 us (1%)
    pallas_call x1, Pallas kernels, body(): pl.pallas_call(kernel, out_shape=jax.ShapeDtypeStruct((OWN, sum(WIDTHS)),...  56.7 us
    unnamed x10, local copies, waits for them, and re-layouts  5.52 us

profile of v1, /device:TPU:6, one launch (start us, length us, event | category | flops | bytes accessed | tf_op | source)
XLA Modules:
  0.0 65.2 jit_solution(4400991416425279132)
XLA Ops:
  0.6 0.0 copy-start
  0.7 1.4 %copy-done = bf16[1024,768]{1,0:T(8,128)(2,1)S(1)} copy-done((bf16[1024,768]{1,0:T(8,128)(2,1)S(1)}, bf16[1024,768]{1,0:T(8,128)(2,1)}, u32[]{:S(2)}) %copy-start) | copy-done | bytes 1572888
  2.0 0.0 copy-start.1
  2.1 1.4 %copy-done.1 = bf16[1024,768]{1,0:T(8,128)(2,1)S(1)} copy-done((bf16[1024,768]{1,0:T(8,128)(2,1)S(1)}, bf16[1024,768]{1,0:T(8,128)(2,1)}, u32[]{:S(2)}) %copy-start.1) | copy-done | bytes 1572888
  3.5 0.0 copy-start.2
  3.5 1.3 %copy-done.2 = bf16[768,768]{1,0:T(8,128)(2,1)S(1)} copy-done((bf16[768,768]{1,0:T(8,128)(2,1)S(1)}, bf16[768,768]{1,0:T(8,128)(2,1)}, u32[]{:S(2)}) %copy-start.2) | copy-done | bytes 1179672
  4.7 0.0 copy-start.3
  4.7 0.8 %copy-done.3 = s32[8192]{0:T(1024)S(1)} copy-done((s32[8192]{0:T(1024)S(1)}, s32[8192]{0:T(1024)}, u32[]{:S(2)}) %copy-start.3) | copy-done | bytes 32792
  5.5 0.0 copy-start.4
  5.5 0.7 %copy-done.4 = s32[1024]{0:T(1024)S(1)} copy-done((s32[1024]{0:T(1024)S(1)}, s32[1024]{0:T(1024)}, u32[]{:S(2)}) %copy-start.4) | copy-done | bytes 4120
  6.2 56.7 %shard_map.77 = f32[16,896]{1,0:T(8,128)S(1)} custom-call(bf16[1024,768]{1,0:T(8,128)(2,1)S(1)} %copy-done.1, bf16[4,8,2,16,768]{4,3,2,1,0:T(8,128)(2,1)S(1)} %bitcast.7, bf16[768,768]{1,0:T(8,128)(2,1)S(1)} %copy-done.2, s32[8,128]{1,0:T(8,128)S(1)} %bitcast.9, s32[8,8,128]{2,1,0:T(8,128)S(1)} %bitcast.8), custom_call_target="tpu_custom_call" | custom-call | tf_op jit(solution)/shard_map/pallas_call | solution.py:332
  62.9 0.2 add_reduce_fusion
  63.1 0.8 %fusion = (f32[16]{0:T(128)S(1)}, f32[16]{0:T(128)S(1)}) fusion(f32[16]{0:T(128)S(1)} %add_reduce_fusion, f32[1024]{0:T(1024)} %param.8, s32[]{:T(128)S(6)} %select_n.4), kind=kLoop, calls=%fused_computation.3 | loop fusion | flops 16 | bytes 260 | tf_op jit(solution)/shard_map/add | solution.py:352
  63.9 0.7 %divide_bitcast_fusion = f32[1,16,768]{2,1,0:T(8,128)} fusion(f32[16,896]{1,0:T(8,128)S(1)} %shard_map.77, f32[16]{0:T(128)S(1)} %get-tuple-element.2, bf16[1024,768]{1,0:T(8,128)(2,1)S(1)} %copy-done, s32[]{:T(128)S(6)} %select_n.4, f32[16]{0:T(128)S(1)} %get-tuple-element.3), kind=kLoop, calls=%fused_computation | loop fusion | flops 49152 | bytes 123012 | tf_op jit(solution)/shard_map/broadcast_in_dim | solution.py:354
  64.6 0.6 multiply_bitcast_fusion
Async XLA Ops:
  0.6 1.4 %copy-start = (bf16[1024,768]{1,0:T(8,128)(2,1)S(1)}, bf16[1024,768]{1,0:T(8,128)(2,1)}, u32[]{:S(2)}) copy-start(bf16[1024,768]{1,0:T(8,128)(2,1)} %param.7) | copy-start | bytes 4718596
  2.0 1.4 %copy-start.1 = (bf16[1024,768]{1,0:T(8,128)(2,1)S(1)}, bf16[1024,768]{1,0:T(8,128)(2,1)}, u32[]{:S(2)}) copy-start(bf16[1024,768]{1,0:T(8,128)(2,1)} %vec_hbm.1) | copy-start | bytes 4718596
  3.5 1.3 %copy-start.2 = (bf16[768,768]{1,0:T(8,128)(2,1)S(1)}, bf16[768,768]{1,0:T(8,128)(2,1)}, u32[]{:S(2)}) copy-start(bf16[768,768]{1,0:T(8,128)(2,1)} %rot_hbm.1) | copy-start | bytes 3538948
  4.7 0.8 %copy-start.3 = (s32[8192]{0:T(1024)S(1)}, s32[8192]{0:T(1024)}, u32[]{:S(2)}) copy-start(s32[8192]{0:T(1024)} %param.10) | copy-start | bytes 98308
  5.5 0.7 %copy-start.4 = (s32[1024]{0:T(1024)S(1)}, s32[1024]{0:T(1024)}, u32[]{:S(2)}) copy-start(s32[1024]{0:T(1024)} %param.9) | copy-start | bytes 12292

commit v2 on v0

v2 whole, which is shorter than its diff:
```python
import contextlib
import math

import jax
import jax.numpy as jnp
from jax import lax
from jax.experimental import pallas as pl
from jax.experimental.pallas import tpu as pltpu
from jax.sharding import Mesh
from jax.sharding import PartitionSpec as P

F32 = jnp.float32
BF16 = jnp.bfloat16
DP = ("dp_0", "dp_1", "dp_2")
NX, NZ, NC, NY = 4, 8, 2, 8
OWN = 16
SUB = 16
WIDTHS = (384, 384, 128)
scope = contextlib.nullcontext


def dot(a, b, dims=((1,), (0,))):
    return lax.dot_general(a, b, (dims, ((), ())), preferred_element_type=F32)


def as_row(a):
    return jnp.concatenate([a[j : j + 1, :] for j in range(a.shape[0])], axis=1)


def as_bf16(mask):
    return mask.astype(F32).astype(BF16)


def iota(shape, dim):
    return lax.broadcasted_iota(jnp.int32, shape, dim)


def kernel(
    vec_hbm, cent_hbm, rot_hbm, prior_hbm, assign_hbm, owner_hbm, new_ref, mom_ref,
    vec, cent, rot, prior, assign, owner, score, prob, weight, moment,
    stat_out, stat_in, rows_out, rows_in, turned_rows,
    own0, own1, own2, snd0, snd1, snd2, rcv0, rcv1, rcv2,
    xs0, xs1, xr0, xr1, zs0, zs1, zs2, zr0, zr1, zr2, last, last_in,
    load_sem, stat_ss, stat_rs, rows_ss, rows_rs, core_ss, core_rs, x_ss, x_rs, z_ss, z_rs,
    last_ss, last_rs,
):
    own, snd, rcv = (own0, own1, own2), (snd0, snd1, snd2), (rcv0, rcv1, rcv2)
    xs, xr, zs, zr = (xs0, xs1), (xr0, xr1), (zs0, zs1, zs2), (zr0, zr1, zr2)
    px, pz, pc = (lax.axis_index(name) for name in DP)
    py = lax.axis_index("cent")
    rows, width = vec.shape
    per_shard = rows // NY
    span = width // NY
    inv_root = 1.0 / math.sqrt(width)

    def load(k, src, dst):
        return pltpu.make_async_copy(src, dst, load_sem.at[k])

    vec_loads = [
        load(9 + k, vec_hbm.at[pl.ds(256 * k, 256)], vec.at[pl.ds(256 * k, 256)]) for k in range(4)
    ]
    cent_loads = [
        load(1 + k, cent_hbm.at[lax.rem(px + k, NX)], cent.at[lax.rem(px + k, NX)])
        for k in range(NX)
    ]
    small_loads = [
        load(5, assign_hbm, assign), load(6, owner_hbm.at[py], owner), load(7, prior_hbm, prior)
    ]
    rot_load = load(8, rot_hbm, rot)
    for item in vec_loads + cent_loads:
        item.start()

    barrier = pltpu.get_barrier_semaphore()
    partners = [{"cent": lax.rem(py + j, NY)} for j in range(1, NY)]
    partners += [{"dp_2": lax.rem(pc + 1, NC)}]
    partners += [{"dp_0": lax.rem(px + j, NX)} for j in range(1, NX)]
    partners += [{"dp_1": lax.rem(pz + j, NZ)} for j in range(1, NZ)]
    for partner in partners:
        pl.semaphore_signal(
            barrier, inc=1, device_id=partner, device_id_type=pl.DeviceIdType.MESH
        )

    def remote(src, dst, ss, rs, device):
        return pltpu.make_async_remote_copy(
            src_ref=src, dst_ref=dst, send_sem=ss, recv_sem=rs,
            device_id=device, device_id_type=pl.DeviceIdType.MESH,
        )

    with scope("loadwait"):
        for item in vec_loads:
            item.wait()
    for item in small_loads + [rot_load]:
        item.start()
    tops = []
    with scope("score"):
        for rx in range(NX):
            cent_loads[rx].wait()
            blocks = [
                cent[lax.rem(px + rx, NX), lax.rem(pz + rz, NZ), lax.rem(pc + rc, NC)]
                for rc in range(NC)
                for rz in range(NZ)
            ]
            lhs = jnp.concatenate(blocks, axis=0)
            wide = lhs.astype(F32)
            square = jnp.sum(wide * wide, axis=1, keepdims=True)
            got = (2.0 * dot(lhs, vec[...], ((1,), (1,))) - square) * inv_root
            top = jnp.max(jnp.max(got.reshape(32, 8, rows), axis=0), axis=0, keepdims=True)
            if rx:
                top = jnp.maximum(top, tops[-1])
            got = jnp.exp(got - top)
            for rc in range(NC):
                at = 512 * rc + 128 * rx
                score[at : at + 128, :] = got[128 * rc : 128 * (rc + 1)]
            part = jnp.sum(got.reshape(32, 8, rows), axis=0)
            total = part + total * jnp.exp(tops[-1] - top) if rx else part
            tops.append(top)
    level = tops[-1] + jnp.log(jnp.sum(total, axis=0, keepdims=True))
    for j in range(8):
        stat_out[j : j + 1, :] = level[:, 128 * j : 128 * (j + 1)]

    with scope("barrier"):
        pl.semaphore_wait(barrier, len(partners))
    stat_copies = [
        remote(stat_out, stat_in.at[j - 1], stat_ss.at[j - 1], stat_rs.at[j - 1],
               {"cent": lax.rem(py + j, NY)})
        for j in range(1, NY)
    ]
    for copy in stat_copies:
        copy.start()

    with scope("rows"):
        for item in small_loads:
            item.wait()
        lists = assign[...]
        inside = lax.shift_right_logical(lists, 10) == py
        flag = as_bf16(inside)
        before = dot(flag, as_bf16(iota((128, 128), 0) < iota((128, 128), 1)))
        whole = dot(flag, jnp.ones((128, 128), BF16)).astype(BF16)
        earlier = dot(as_bf16(iota((8, 8), 1) < iota((8, 8), 0)), whole)
        rank = jnp.where(inside, before + earlier, -1.0)
        local = jnp.bitwise_and(lists, 1023).astype(F32)
        pick = iota((per_shard, rows), 0).astype(F32) == as_row(rank)
        list_of = jnp.sum(jnp.where(pick, as_row(local), 0.0), axis=1, keepdims=True)
        member = iota((per_shard, rows), 1).astype(F32) == list_of
        holder = as_row(owner[...].astype(F32))
        owner_col = jnp.sum(jnp.where(member, holder, 0.0), axis=1, keepdims=True)
        vec_rows = dot(as_bf16(pick), vec[...])
        cent_rows = dot(as_bf16(member), cent[...].reshape(rows, width))
        residual = (vec_rows - cent_rows).astype(BF16)
        rot_load.wait()
        turned = dot(residual, rot[...])
        owner_wide = jnp.broadcast_to(owner_col, (per_shard, 128))
        turned = jnp.concatenate([turned, owner_wide], axis=1).T.astype(BF16)
        for c in range(NY):
            rows_out[c, 0:span] = turned[span * c : span * (c + 1)]
            rows_out[c, span : span + 16] = turned[width : width + 16]
    row_copies = [
        remote(rows_out.at[lax.rem(py + j, NY)], rows_in.at[j - 1],
               rows_ss.at[j - 1], rows_rs.at[j - 1], {"cent": lax.rem(py + j, NY)})
        for j in range(1, NY)
    ]
    for copy in row_copies:
        copy.start()

    with scope("statwait"):
        for copy in stat_copies:
            copy.wait_recv()
    levels = [stat_out[...]] + [stat_in[j] for j in range(NY - 1)]
    peak = levels[0]
    for item in levels[1:]:
        peak = jnp.maximum(peak, item)
    whole_total = jnp.exp(levels[0] - peak)
    for item in levels[1:]:
        whole_total += jnp.exp(item - peak)
    peak, whole_total = as_row(peak), as_row(whole_total)

    sibling = {"dp_2": lax.rem(pc + 1, NC)}
    x_side = [{"dp_0": lax.rem(px + j, NX)} for j in (1, NX - 1)]

    def core_copy(q, rx):
        k = q * NX + rx
        at = pl.ds(128 * rx, 128)
        return remote(snd[q].at[at], rcv[q].at[at], core_ss.at[k], core_rs.at[k], sibling)

    moment_copy = remote(snd[2], rcv[2], core_ss.at[8], core_rs.at[8], sibling)

    def x_copy(q, j):
        k = q * 6 + j
        return remote(xs[q].at[j], xr[q].at[j], x_ss.at[k], x_rs.at[k], x_side[j % 2])

    def z_copy(q, j):
        k = q * (NZ - 1) + j - 1
        return remote(zs[q].at[j - 1], zr[q].at[j - 1], z_ss.at[k], z_rs.at[k],
                      {"dp_1": lax.rem(pz + j, NZ)})

    def last_copy(j):
        return remote(last.at[j], last_in.at[j - 1], last_ss.at[j - 1], last_rs.at[j - 1],
                      {"dp_0": lax.rem(px + j, NX)})

    def sums(rx):
        at, sent = slice(128 * rx, 128 * (rx + 1)), slice(512 + 128 * rx, 640 + 128 * rx)
        factor = jnp.exp(tops[rx] - peak) / whole_total
        for side in (sent, at):
            got = score[side, :] * factor
            prob[side, :] = got.astype(BF16)
            parts = [got[:, 128 * j : 128 * (j + 1)] for j in range(8)]
            while len(parts) > 1:
                parts = [a + b for a, b in zip(parts[::2], parts[1::2])]
            weight[side, :] = parts[0]
        got = dot(jnp.concatenate([prob[sent, :], prob[at, :]], axis=0), vec[...])
        for q in range(2):
            snd[q][at, :] = got[:128, 384 * q : 384 * (q + 1)].astype(BF16)
            core_copy(q, rx).start()
        for q in range(2):
            own[q][at, :] = got[128:, 384 * q : 384 * (q + 1)]

    def split_mass(a):
        lane = iota(a.shape, 1)
        mass = jnp.where((lane >= span) & (lane < span + 2), a, 0.0)
        mass = jnp.sum(mass, axis=1, keepdims=True)
        high = mass.astype(BF16).astype(F32)
        return jnp.where(lane == span, high, jnp.where(lane == span + 1, mass - high, a))

    def moments():
        for copy in row_copies:
            copy.wait_recv()
        got = jnp.concatenate([rows_out[py]] + [rows_in[j] for j in range(NY - 1)], axis=1)
        turned_rows[...] = got[0:span].astype(F32)
        holders = got[span : span + 1].astype(F32)
        q = iota((64, 1), 0)
        qc, qx, qz = q // 32, (q // 8) % 4, q % 8
        wanted = (((px + qx) % NX) * NZ + (pz + qz) % NZ) * NC + (pc + qc) % NC
        chosen = as_bf16(wanted.astype(F32) == holders)
        filler = jnp.zeros((128 - span, rows), BF16)
        by_owner = moment.reshape(64, OWN, 128)
        for pair in range(SUB // 2):
            pieces = []
            for a in (2 * pair, 2 * pair + 1):
                for m in range(span // SUB):
                    block = turned_rows[SUB * m : SUB * (m + 1), :]
                    line = turned_rows[SUB * m + a : SUB * m + a + 1, :]
                    pieces.append((block * line).astype(BF16))
                pieces.append(filler)
            both = dot(chosen, jnp.concatenate(pieces, axis=0), ((1,), (1,)))
            for side in range(2):
                by_owner[:, 2 * pair + side, :] = both[:, 128 * side : 128 * (side + 1)]
        mass = jnp.sum(weight[...], axis=1, keepdims=True)
        both = split_mass(moment[...] + jnp.where(iota((rows, 128), 1) == span, mass, 0.0))
        snd[2][...] = both[512:].astype(BF16)
        moment_copy.start()
        own[2][...] = both[:512]

    def joined(q, rx):
        core_copy(q, rx).wait_recv()
        at = slice(128 * rx, 128 * (rx + 1))
        return own[q][at, :] + rcv[q][at, :].astype(F32)

    def x_far(q):
        got = joined(q, 2).astype(BF16)
        for side in range(2):
            xs[q][side] = got[64 * side : 64 * (side + 1)]
            x_copy(q, side).start()

    def x_plain(q, side):
        got = joined(q, (1, 3)[side])
        plain, rest = (got[64:], got[:64]) if side == 0 else (got[:64], got[64:])
        xs[q][2 + side] = plain.astype(BF16)
        x_copy(q, 2 + side).start()
        own[q][128 * (1 + side) : 128 * (1 + side) + 64, :] = rest

    def x_add(q):
        for side in range(2):
            x_copy(q, side).wait_recv()
            rest = own[q][128 * (1 + side) : 128 * (1 + side) + 64, :]
            xs[q][4 + side] = (rest + xr[q][side].astype(F32)).astype(BF16)
            x_copy(q, 4 + side).start()

    def near(q):
        own[q][0:128, :] = joined(q, 0)

    def z_send(q):
        for j in (2, 3, 4, 5):
            x_copy(q, j).wait_recv()
        low = own[q][0:64, :] + xr[q][4].astype(F32) + xr[q][3].astype(F32)
        high = own[q][64:128, :] + xr[q][2].astype(F32) + xr[q][5].astype(F32)
        block = [part[16 * j : 16 * (j + 1)] for part in (low, high) for j in range(4)]
        for j in (4, 3, 5, 2, 6, 1, 7):
            zs[q][j - 1] = block[j].astype(BF16)
            z_copy(q, j).start()
        own[q][0:OWN, :] = block[0]

    def finish(q):
        got = own[q][0:OWN, :]
        for j in (1, 7, 2, 6, 3, 5, 4):
            z_copy(q, j).wait_recv()
            got = got + zr[q][j - 1].astype(F32)
        return got

    def moments_z():
        moment_copy.wait_recv()
        got = split_mass(own[2][...] + rcv[2][...].astype(F32)).reshape(NX, NZ, OWN, 128)
        for j in (4, 3, 5, 2, 6, 1, 7):
            zs[2][j - 1] = got[:, j].astype(BF16)
            z_copy(2, j).start()
        last[...] = got[:, 0]

    def moments_x():
        got = last[...]
        for j in (1, 7, 2, 6, 3, 5, 4):
            z_copy(2, j).wait_recv()
            got = got + zr[2][j - 1].astype(F32)
        last[...] = got
        for j in (2, 1, 3):
            last_copy(j).start()

    def moments_end():
        got = last[0]
        for j in range(1, NX):
            last_copy(j).wait_recv()
            got = got + last_in[j - 1]
        return got

    def staged(stage, *at):
        with scope(stage.__name__ + "".join(map(str, at))):
            return stage(*at)

    staged(sums, 2)
    staged(sums, 1)
    staged(x_far, 0)
    staged(x_far, 1)
    staged(sums, 3)
    staged(x_plain, 0, 0)
    staged(x_plain, 1, 0)
    staged(sums, 0)
    staged(x_plain, 0, 1)
    staged(x_plain, 1, 1)
    staged(moments)
    staged(near, 0)
    staged(near, 1)
    staged(x_add, 0)
    staged(x_add, 1)
    staged(moments_z)
    staged(z_send, 0)
    staged(z_send, 1)
    staged(moments_x)
    parts = [staged(finish, 0), staged(finish, 1), staged(moments_end)]
    lane = iota((OWN, 128), 1)
    mass = jnp.sum(
        jnp.where((lane >= span) & (lane < span + 2), parts[2], 0.0), axis=1, keepdims=True
    )
    first = ((px * NZ + pz) * NC + pc) * OWN
    mine = iota((OWN, rows), 1) == iota((OWN, rows), 0) + first
    prior_col = jnp.sum(jnp.where(mine, as_row(prior[...]), 0.0), axis=1, keepdims=True)
    own_cent = cent[px, pz, pc].astype(F32)
    new_ref[...] = (prior_col * own_cent + jnp.concatenate(parts[:2], axis=1)) / (prior_col + mass)
    mom_ref[...] = parts[2][:, :span] / rows

    with scope("endwaits"):
        for copy in stat_copies + row_copies:
            copy.wait_send()
        moment_copy.wait_send()
        for q in range(2):
            for rx in range(NX):
                core_copy(q, rx).wait_send()
            for j in range(6):
                x_copy(q, j).wait_send()
        for j in range(1, NX):
            last_copy(j).wait_send()
        for q in range(3):
            for j in range(1, NZ):
                z_copy(q, j).wait_send()


def body(vectors, centroids, prior_mass, assign, owner_of, rotation):
    rows, width = vectors.shape
    span = width // NY
    half = rows // 2
    any_spec = pl.BlockSpec(memory_space=pl.ANY)
    vmem_spec = pl.BlockSpec(memory_space=pltpu.VMEM)
    dma = pltpu.SemaphoreType.DMA
    scratch = [
        pltpu.VMEM((rows, width), BF16),
        pltpu.VMEM((NX, NZ, NC, OWN, width), BF16),
        pltpu.VMEM((width, width), BF16),
        pltpu.VMEM((8, 128), F32),
        pltpu.VMEM((8, 128), jnp.int32),
        pltpu.VMEM((8, 128), jnp.int32),
        pltpu.VMEM((rows, rows), F32),
        pltpu.VMEM((rows, rows), BF16),
        pltpu.VMEM((rows, 128), F32),
        pltpu.VMEM((rows, 128), F32),
        pltpu.VMEM((8, 128), F32),
        pltpu.VMEM((NY - 1, 8, 128), F32),
        pltpu.VMEM((NY, span + 16, 128), BF16),
        pltpu.VMEM((NY - 1, span + 16, 128), BF16),
        pltpu.VMEM((span, rows), F32),
    ]
    scratch += [pltpu.VMEM((half, w), F32) for w in WIDTHS]
    scratch += [pltpu.VMEM((half, w), BF16) for w in WIDTHS] * 2
    scratch += [pltpu.VMEM((6, 64, w), BF16) for w in WIDTHS[:2]] * 2
    turns = [pltpu.VMEM((NZ - 1, OWN, w), BF16) for w in WIDTHS[:2]]
    turns += [pltpu.VMEM((NZ - 1, NX, OWN, 128), BF16)]
    scratch += turns * 2 + [pltpu.VMEM((NX, OWN, 128), F32), pltpu.VMEM((NX - 1, OWN, 128), F32)]
    scratch += [dma((13,))] + [dma((7,))] * 4 + [dma((9,))] * 2 + [dma((12,))] * 2 + [dma((21,))] * 2
    scratch += [dma((3,))] * 2
    updated, moments = pl.pallas_call(
        kernel,
        out_shape=(
            jax.ShapeDtypeStruct((OWN, width), F32),
            jax.ShapeDtypeStruct((OWN, span), F32),
        ),
        in_specs=[any_spec] * 6,
        out_specs=(vmem_spec, vmem_spec),
        scratch_shapes=scratch,
        compiler_params=pltpu.CompilerParams(
            collective_id=0, has_side_effects=True, vmem_limit_bytes=40000 * 1024
        ),
    )(*(pltpu.with_memory_space_constraint(a, pltpu.HBM) for a in (
        vectors,
        centroids.reshape(NX, NZ, NC, OWN, width),
        rotation,
        prior_mass.reshape(8, 128),
        assign.reshape(8, 128),
        owner_of.reshape(NY, 8, 128),
    )))
    return (updated[None], moments[None])


def solution(mesh):
    finer = Mesh(
        mesh.devices.reshape(NX, NZ, NC, mesh.shape["cent"]), ("dp_0", "dp_1", "dp_2", "cent")
    )
    in_specs = (P(DP, None), P("cent", None), P("cent"), P(DP), P(), P())
    out_specs = (P("cent", DP, None), P(DP, None, "cent"))
    return jax.shard_map(body, mesh=finer, in_specs=in_specs, out_specs=out_specs, check_vma=False)
```

time: 156 us -> 42.3 us (0.27); the launches traced: 154 us -> 42.2 us
  waiting for transfers between devices: 57 us -> 0 us
  Pallas kernels: 0 us -> 40.3 us
  starting transfers between devices: 40 us -> 0 us
  local copies, waits for them, and re-layouts: 27.8 us -> 1.22 us
  other arithmetic: 19.1 us -> 0 us
  matrix products: 8.69 us -> 0 us
    all_to_all x5 -> x0, waiting for transfers between devices: 57 us -> none  [the longest x1 42 us: sum_by_axis(): return jnp.sum(lax.all_to_all(own, far, 0, 0, tiled=True), axis=0)]
    pallas_call x0 -> x1, Pallas kernels: none -> 40.3 us  [body(): pl.pallas_call(kernel, out_shape=(jax.ShapeDtypeStruct((OWN, width), F32)...]
    all_to_all x5 -> x0, starting transfers between devices: 40 us -> none  [the longest x1 14.3 us: body(): lax.all_to_all(packed, DP, split_axis=0, concat_axis=0, tiled=True)]
    reshape x3 -> x0, local copies, waits for them, and re-layouts: 12.3 us -> none  [the longest x2 12.3 us: body(): flat_rows = rotated.reshape(owner_count * slot_cap, M, sub_width)]
    reduce_sum x7 -> x0, other arithmetic: 11.8 us -> none  [the longest x1 4.87 us: body(): soft_mass = jnp.sum(member_prob, axis=0, dtype=jnp.float32)]
    dot_general x4 -> x0, matrix products: 8.69 us -> none  [the longest x1 3.38 us: body(): lax.dot_general(member_prob, vectors, (((0,), (0,)), ((), ())), preferred...]
    scatter x2 -> x0, local copies, waits for them, and re-layouts: 6.4 us -> none  [the longest x1 4.3 us: body(): picked = jnp.zeros((per_shard,), jnp.int32).at[target].set(jnp.arange(row...]
    gather x4 -> x0, local copies, waits for them, and re-layouts: 4.53 us -> none  [the longest x1 1.54 us: body(): centroids[local_list].astype(jnp.float32)]
  transfers between devices with their start and end apart: 5 -> 0, of which waited for: 3 -> 0; matrix products, arithmetic and copies ran while one was open for 29% -> 0% of each run, Pallas kernels for 0% -> 0%
where the time goes in v2:
time: 42.3 us; the launch traced here: 42.2 us
  Pallas kernels  40.3 us (95%)
  local copies, waits for them, and re-layouts  1.22 us (3%)
  between operations  0.64 us (2%)
    pallas_call x1, Pallas kernels, body(): pl.pallas_call(kernel, out_shape=(jax.ShapeDtypeStruct((OWN, width), F32)...  40.3 us
    unnamed x2, local copies, waits for them, and re-layouts  1.22 us

profile of v2, /device:TPU:1, one launch (start us, length us, event | category | flops | bytes accessed | tf_op | source)
XLA Modules:
  0.0 42.2 jit_solution(18096224647800575796)
XLA Ops:
  0.6 40.3 %shard_map.77 = (f32[16,768]{1,0:T(8,128)S(1)}, f32[16,96]{1,0:T(8,128)S(1)}) custom-call(bf16[1024,768]{1,0:T(8,128)(2,1)} %vec_hbm.1, bf16[4,8,2,16,768]{4,3,2,1,0:T(8,128)(2,1)} %bitcast.8, bf16[768,768]{1,0:T(8,128)(2,1)} %rot_hbm.1, f32[8,128]{1,0:T(8,128)} %bitcast.10, s32[8,128]{1,0:T(8,128)} %bitcast.11, s32[8,8,128]{2,1,0:T(8,128)} %bitcast.9), custom_call_target="tpu_custom_call" | custom-call | tf_op jit(solution)/shard_map/pallas_call | solution.py:406
  40.9 0.6 %copy.10 = f32[1,16,768]{2,1,0:T(8,128)} copy(f32[1,16,768]{2,1,0:T(8,128)S(1)} %bitcast.6) | data formatting | bytes 98304
  41.6 0.6 %copy.11 = f32[1,16,96]{2,1,0:T(8,128)} copy(f32[1,16,96]{2,1,0:T(8,128)S(1)} %bitcast.7) | data formatting | bytes 12288

commit v3 on v2

--- a/solution.py
+++ b/solution.py
@@ -15,7 +15,6 @@
 NX, NZ, NC, NY = 4, 8, 2, 8
 OWN = 16
 SUB = 16
-WIDTHS = (384, 384, 128)
 scope = contextlib.nullcontext
 
 
@@ -39,12 +38,10 @@
     vec_hbm, cent_hbm, rot_hbm, prior_hbm, assign_hbm, owner_hbm, new_ref, mom_ref,
     vec, cent, rot, prior, assign, owner, score, prob, weight, moment,
     stat_out, stat_in, rows_out, rows_in, turned_rows,
-    own0, own1, own2, snd0, snd1, snd2, rcv0, rcv1, rcv2,
+    own, own_m, snd, snd_m, rcv, rcv_m,
     xs0, xs1, xr0, xr1, zs0, zs1, zs2, zr0, zr1, zr2, last, last_in,
-    load_sem, stat_ss, stat_rs, rows_ss, rows_rs, core_ss, core_rs, x_ss, x_rs, z_ss, z_rs,
-    last_ss, last_rs,
+    load_sem, send_sem, recv_sem,
 ):
-    own, snd, rcv = (own0, own1, own2), (snd0, snd1, snd2), (rcv0, rcv1, rcv2)
     xs, xr, zs, zr = (xs0, xs1), (xr0, xr1), (zs0, zs1, zs2), (zr0, zr1, zr2)
     px, pz, pc = (lax.axis_index(name) for name in DP)
     py = lax.axis_index("cent")
@@ -56,19 +53,20 @@
     def load(k, src, dst):
         return pltpu.make_async_copy(src, dst, load_sem.at[k])
 
-    vec_loads = [
-        load(9 + k, vec_hbm.at[pl.ds(256 * k, 256)], vec.at[pl.ds(256 * k, 256)]) for k in range(4)
-    ]
+    def wait_all(ref, sem):
+        pltpu.make_async_copy(ref, ref, sem).wait()
+
     cent_loads = [
-        load(1 + k, cent_hbm.at[lax.rem(px + k, NX)], cent.at[lax.rem(px + k, NX)])
+        load(k, cent_hbm.at[lax.rem(px + k, NX)], cent.at[lax.rem(px + k, NX)])
         for k in range(NX)
     ]
     small_loads = [
         load(5, assign_hbm, assign), load(6, owner_hbm.at[py], owner), load(7, prior_hbm, prior)
     ]
     rot_load = load(8, rot_hbm, rot)
-    for item in vec_loads + cent_loads:
-        item.start()
+    for k in range(4):
+        load(4, vec_hbm.at[pl.ds(256 * k, 256)], vec.at[pl.ds(256 * k, 256)]).start()
+    cent_loads[0].start()
 
     barrier = pltpu.get_barrier_semaphore()
     partners = [{"cent": lax.rem(py + j, NY)} for j in range(1, NY)]
@@ -80,40 +78,49 @@
             barrier, inc=1, device_id=partner, device_id_type=pl.DeviceIdType.MESH
         )
 
+    for item in cent_loads[1:]:
+        item.start()
+
     def remote(src, dst, ss, rs, device):
         return pltpu.make_async_remote_copy(
-            src_ref=src, dst_ref=dst, send_sem=ss, recv_sem=rs,
+            src_ref=src, dst_ref=dst, send_sem=send_sem.at[ss], recv_sem=recv_sem.at[rs],
             device_id=device, device_id_type=pl.DeviceIdType.MESH,
         )
 
     with scope("loadwait"):
-        for item in vec_loads:
-            item.wait()
+        wait_all(vec, load_sem.at[4])
     for item in small_loads + [rot_load]:
         item.start()
-    tops = []
+    tops, total = [], None
     with scope("score"):
-        for rx in range(NX):
-            cent_loads[rx].wait()
-            blocks = [
-                cent[lax.rem(px + rx, NX), lax.rem(pz + rz, NZ), lax.rem(pc + rc, NC)]
-                for rc in range(NC)
-                for rz in range(NZ)
-            ]
-            lhs = jnp.concatenate(blocks, axis=0)
-            wide = lhs.astype(F32)
-            square = jnp.sum(wide * wide, axis=1, keepdims=True)
-            got = (2.0 * dot(lhs, vec[...], ((1,), (1,))) - square) * inv_root
-            top = jnp.max(jnp.max(got.reshape(32, 8, rows), axis=0), axis=0, keepdims=True)
-            if rx:
-                top = jnp.maximum(top, tops[-1])
-            got = jnp.exp(got - top)
-            for rc in range(NC):
-                at = 512 * rc + 128 * rx
-                score[at : at + 128, :] = got[128 * rc : 128 * (rc + 1)]
-            part = jnp.sum(got.reshape(32, 8, rows), axis=0)
-            total = part + total * jnp.exp(tops[-1] - top) if rx else part
-            tops.append(top)
+        cent_loads[0].wait()
+        for rx in range(NX + 1):
+            if rx < NX:
+                blocks = [
+                    cent[lax.rem(px + rx, NX), lax.rem(pz + rz, NZ), lax.rem(pc + rc, NC)]
+                    for rc in range(NC)
+                    for rz in range(NZ)
+                ]
+                lhs = jnp.concatenate(blocks, axis=0)
+                wide = lhs.astype(F32)
+                square = jnp.sum(wide * wide, axis=1, keepdims=True)
+                got = (2.0 * dot(lhs, vec[...], ((1,), (1,))) - square) * inv_root
+                for rc in range(NC):
+                    at = 512 * rc + 128 * rx
+                    score[at : at + 128, :] = got[128 * rc : 128 * (rc + 1)]
+                top = jnp.max(jnp.max(got.reshape(32, 8, rows), axis=0), axis=0, keepdims=True)
+                tops.append(jnp.maximum(top, tops[-1]) if rx else top)
+            if rx == 0:
+                for item in cent_loads[1:]:
+                    item.wait()
+            else:
+                top, part = tops[rx - 1], jnp.zeros((8, rows), F32)
+                for rc in range(NC):
+                    at = 512 * rc + 128 * (rx - 1)
+                    got = jnp.exp(score[at : at + 128, :] - top)
+                    score[at : at + 128, :] = got
+                    part = part + jnp.sum(got.reshape(16, 8, rows), axis=0)
+                total = part + total * jnp.exp(tops[rx - 2] - top) if rx > 1 else part
     level = tops[-1] + jnp.log(jnp.sum(total, axis=0, keepdims=True))
     for j in range(8):
         stat_out[j : j + 1, :] = level[:, 128 * j : 128 * (j + 1)]
@@ -121,7 +128,7 @@
     with scope("barrier"):
         pl.semaphore_wait(barrier, len(partners))
     stat_copies = [
-        remote(stat_out, stat_in.at[j - 1], stat_ss.at[j - 1], stat_rs.at[j - 1],
+        remote(stat_out, stat_in.at[j - 1], 0, 0,
                {"cent": lax.rem(py + j, NY)})
         for j in range(1, NY)
     ]
@@ -156,15 +163,14 @@
             rows_out[c, span : span + 16] = turned[width : width + 16]
     row_copies = [
         remote(rows_out.at[lax.rem(py + j, NY)], rows_in.at[j - 1],
-               rows_ss.at[j - 1], rows_rs.at[j - 1], {"cent": lax.rem(py + j, NY)})
+               1, 1, {"cent": lax.rem(py + j, NY)})
         for j in range(1, NY)
     ]
     for copy in row_copies:
         copy.start()
 
     with scope("statwait"):
-        for copy in stat_copies:
-            copy.wait_recv()
+        wait_all(stat_in, recv_sem.at[0])
     levels = [stat_out[...]] + [stat_in[j] for j in range(NY - 1)]
     peak = levels[0]
     for item in levels[1:]:
@@ -177,25 +183,21 @@
     sibling = {"dp_2": lax.rem(pc + 1, NC)}
     x_side = [{"dp_0": lax.rem(px + j, NX)} for j in (1, NX - 1)]
 
-    def core_copy(q, rx):
-        k = q * NX + rx
+    def core_copy(rx):
         at = pl.ds(128 * rx, 128)
-        return remote(snd[q].at[at], rcv[q].at[at], core_ss.at[k], core_rs.at[k], sibling)
-
-    moment_copy = remote(snd[2], rcv[2], core_ss.at[8], core_rs.at[8], sibling)
+        return remote(snd.at[at], rcv.at[at], 10 + rx, 2 + rx, sibling)
+
+    moment_copy = remote(snd_m, rcv_m, 3, 6, sibling)
 
     def x_copy(q, j):
-        k = q * 6 + j
-        return remote(xs[q].at[j], xr[q].at[j], x_ss.at[k], x_rs.at[k], x_side[j % 2])
+        return remote(xs[q].at[j], xr[q].at[j], 4 + q, 7 + 2 * q + (j > 1), x_side[j % 2])
 
     def z_copy(q, j):
-        k = q * (NZ - 1) + j - 1
-        return remote(zs[q].at[j - 1], zr[q].at[j - 1], z_ss.at[k], z_rs.at[k],
+        return remote(zs[q].at[j - 1], zr[q].at[j - 1], 6 + q, 11 + q,
                       {"dp_1": lax.rem(pz + j, NZ)})
 
     def last_copy(j):
-        return remote(last.at[j], last_in.at[j - 1], last_ss.at[j - 1], last_rs.at[j - 1],
-                      {"dp_0": lax.rem(px + j, NX)})
+        return remote(last.at[j], last_in.at[j - 1], 9, 14, {"dp_0": lax.rem(px + j, NX)})
 
     def sums(rx):
         at, sent = slice(128 * rx, 128 * (rx + 1)), slice(512 + 128 * rx, 640 + 128 * rx)
@@ -208,11 +210,9 @@
                 parts = [a + b for a, b in zip(parts[::2], parts[1::2])]
             weight[side, :] = parts[0]
         got = dot(jnp.concatenate([prob[sent, :], prob[at, :]], axis=0), vec[...])
-        for q in range(2):
-            snd[q][at, :] = got[:128, 384 * q : 384 * (q + 1)].astype(BF16)
-            core_copy(q, rx).start()
-        for q in range(2):
-            own[q][at, :] = got[128:, 384 * q : 384 * (q + 1)]
+        snd[at, :] = got[:128].astype(BF16)
+        core_copy(rx).start()
+        own[at, :] = got[128:]
 
     def split_mass(a):
         lane = iota(a.shape, 1)
@@ -222,8 +222,7 @@
         return jnp.where(lane == span, high, jnp.where(lane == span + 1, mass - high, a))
 
     def moments():
-        for copy in row_copies:
-            copy.wait_recv()
+        wait_all(rows_in, recv_sem.at[1])
         got = jnp.concatenate([rows_out[py]] + [rows_in[j] for j in range(NY - 1)], axis=1)
         turned_rows[...] = got[0:span].astype(F32)
         holders = got[span : span + 1].astype(F32)
@@ -246,59 +245,63 @@
                 by_owner[:, 2 * pair + side, :] = both[:, 128 * side : 128 * (side + 1)]
         mass = jnp.sum(weight[...], axis=1, keepdims=True)
         both = split_mass(moment[...] + jnp.where(iota((rows, 128), 1) == span, mass, 0.0))
-        snd[2][...] = both[512:].astype(BF16)
+        snd_m[...] = both[512:].astype(BF16)
         moment_copy.start()
-        own[2][...] = both[:512]
-
-    def joined(q, rx):
-        core_copy(q, rx).wait_recv()
+        own_m[...] = both[:512]
+
+    def joined(rx):
+        core_copy(rx).wait_recv()
         at = slice(128 * rx, 128 * (rx + 1))
-        return own[q][at, :] + rcv[q][at, :].astype(F32)
-
-    def x_far(q):
-        got = joined(q, 2).astype(BF16)
+        return own[at, :] + rcv[at, :].astype(F32)
+
+    def columns(q):
+        return slice(384 * q, 384 * (q + 1))
+
+    def x_far():
+        got = joined(2).astype(BF16)
+        for q in range(2):
+            for side in range(2):
+                xs[q][side] = got[64 * side : 64 * (side + 1), columns(q)]
+                x_copy(q, side).start()
+
+    def x_plain(side):
+        got = joined((1, 3)[side])
+        plain, rest = (got[64:], got[:64]) if side == 0 else (got[:64], got[64:])
+        for q in range(2):
+            xs[q][2 + side] = plain[:, columns(q)].astype(BF16)
+            x_copy(q, 2 + side).start()
+        own[128 * (1 + side) : 128 * (1 + side) + 64, :] = rest
+
+    def near():
+        own[0:128, :] = joined(0)
+
+    def x_add(q):
+        wait_all(xr[q].at[pl.ds(0, 2)], recv_sem.at[7 + 2 * q])
         for side in range(2):
-            xs[q][side] = got[64 * side : 64 * (side + 1)]
-            x_copy(q, side).start()
-
-    def x_plain(q, side):
-        got = joined(q, (1, 3)[side])
-        plain, rest = (got[64:], got[:64]) if side == 0 else (got[:64], got[64:])
-        xs[q][2 + side] = plain.astype(BF16)
-        x_copy(q, 2 + side).start()
-        own[q][128 * (1 + side) : 128 * (1 + side) + 64, :] = rest
-
-    def x_add(q):
-        for side in range(2):
-            x_copy(q, side).wait_recv()
-            rest = own[q][128 * (1 + side) : 128 * (1 + side) + 64, :]
+            rest = own[128 * (1 + side) : 128 * (1 + side) + 64, columns(q)]
             xs[q][4 + side] = (rest + xr[q][side].astype(F32)).astype(BF16)
             x_copy(q, 4 + side).start()
 
-    def near(q):
-        own[q][0:128, :] = joined(q, 0)
-
     def z_send(q):
-        for j in (2, 3, 4, 5):
-            x_copy(q, j).wait_recv()
-        low = own[q][0:64, :] + xr[q][4].astype(F32) + xr[q][3].astype(F32)
-        high = own[q][64:128, :] + xr[q][2].astype(F32) + xr[q][5].astype(F32)
+        wait_all(xr[q].at[pl.ds(2, 4)], recv_sem.at[8 + 2 * q])
+        low = own[0:64, columns(q)] + xr[q][4].astype(F32) + xr[q][3].astype(F32)
+        high = own[64:128, columns(q)] + xr[q][2].astype(F32) + xr[q][5].astype(F32)
         block = [part[16 * j : 16 * (j + 1)] for part in (low, high) for j in range(4)]
         for j in (4, 3, 5, 2, 6, 1, 7):
             zs[q][j - 1] = block[j].astype(BF16)
             z_copy(q, j).start()
-        own[q][0:OWN, :] = block[0]
+        own[0:OWN, columns(q)] = block[0]
 
     def finish(q):
-        got = own[q][0:OWN, :]
-        for j in (1, 7, 2, 6, 3, 5, 4):
-            z_copy(q, j).wait_recv()
-            got = got + zr[q][j - 1].astype(F32)
+        wait_all(zr[q], recv_sem.at[11 + q])
+        got = own[0:OWN, columns(q)]
+        for j in range(NZ - 1):
+            got = got + zr[q][j].astype(F32)
         return got
 
     def moments_z():
         moment_copy.wait_recv()
-        got = split_mass(own[2][...] + rcv[2][...].astype(F32)).reshape(NX, NZ, OWN, 128)
+        got = split_mass(own_m[...] + rcv_m[...].astype(F32)).reshape(NX, NZ, OWN, 128)
         for j in (4, 3, 5, 2, 6, 1, 7):
             zs[2][j - 1] = got[:, j].astype(BF16)
             z_copy(2, j).start()
@@ -306,18 +309,18 @@
 
     def moments_x():
         got = last[...]
-        for j in (1, 7, 2, 6, 3, 5, 4):
-            z_copy(2, j).wait_recv()
-            got = got + zr[2][j - 1].astype(F32)
+        wait_all(zr[2], recv_sem.at[13])
+        for j in range(NZ - 1):
+            got = got + zr[2][j].astype(F32)
         last[...] = got
         for j in (2, 1, 3):
             last_copy(j).start()
 
     def moments_end():
         got = last[0]
-        for j in range(1, NX):
-            last_copy(j).wait_recv()
-            got = got + last_in[j - 1]
+        wait_all(last_in, recv_sem.at[14])
+        for j in range(NX - 1):
+            got = got + last_in[j]
         return got
 
     def staged(stage, *at):
@@ -326,17 +329,13 @@
 
     staged(sums, 2)
     staged(sums, 1)
-    staged(x_far, 0)
-    staged(x_far, 1)
+    staged(x_far)
     staged(sums, 3)
-    staged(x_plain, 0, 0)
-    staged(x_plain, 1, 0)
+    staged(x_plain, 0)
     staged(sums, 0)
-    staged(x_plain, 0, 1)
-    staged(x_plain, 1, 1)
+    staged(x_plain, 1)
+    staged(near)
     staged(moments)
-    staged(near, 0)
-    staged(near, 1)
     staged(x_add, 0)
     staged(x_add, 1)
     staged(moments_z)
@@ -356,19 +355,12 @@
     mom_ref[...] = parts[2][:, :span] / rows
 
     with scope("endwaits"):
-        for copy in stat_copies + row_copies:
-            copy.wait_send()
-        moment_copy.wait_send()
-        for q in range(2):
-            for rx in range(NX):
-                core_copy(q, rx).wait_send()
-            for j in range(6):
-                x_copy(q, j).wait_send()
-        for j in range(1, NX):
-            last_copy(j).wait_send()
-        for q in range(3):
-            for j in range(1, NZ):
-                z_copy(q, j).wait_send()
+        sent = (stat_in, rows_in, snd, snd_m, xs0, xs1, zs0, zs1, zs2, last_in)
+        for k, ref in enumerate(sent):
+            if k != 2:
+                wait_all(ref, send_sem.at[k])
+        for rx in range(NX):
+            core_copy(rx).wait_send()
 
 
 def body(vectors, centroids, prior_mass, assign, owner_of, rotation):
@@ -395,14 +387,12 @@
         pltpu.VMEM((NY - 1, span + 16, 128), BF16),
         pltpu.VMEM((span, rows), F32),
     ]
-    scratch += [pltpu.VMEM((half, w), F32) for w in WIDTHS]
-    scratch += [pltpu.VMEM((half, w), BF16) for w in WIDTHS] * 2
-    scratch += [pltpu.VMEM((6, 64, w), BF16) for w in WIDTHS[:2]] * 2
-    turns = [pltpu.VMEM((NZ - 1, OWN, w), BF16) for w in WIDTHS[:2]]
+    scratch += [pltpu.VMEM((half, w), kind) for kind in (F32, BF16, BF16) for w in (width, 128)]
+    scratch += [pltpu.VMEM((6, 64, 384), BF16)] * 4
+    turns = [pltpu.VMEM((NZ - 1, OWN, 384), BF16)] * 2
     turns += [pltpu.VMEM((NZ - 1, NX, OWN, 128), BF16)]
     scratch += turns * 2 + [pltpu.VMEM((NX, OWN, 128), F32), pltpu.VMEM((NX - 1, OWN, 128), F32)]
-    scratch += [dma((13,))] + [dma((7,))] * 4 + [dma((9,))] * 2 + [dma((12,))] * 2 + [dma((21,))] * 2
-    scratch += [dma((3,))] * 2
+    scratch += [dma((9,)), dma((14,)), dma((15,))]
     updated, moments = pl.pallas_call(
         kernel,
         out_shape=(

time: 42.3 us -> 40.9 us (0.967)
  Pallas kernels: 40.3 us -> 38.9 us
    pallas_call x1, Pallas kernels: 40.3 us -> 38.9 us  [body(): pl.pallas_call(kernel, out_shape=(jax.ShapeDtypeStruct((OWN, width), F32)...]
where the time goes in v3:
time: 40.9 us; the launch traced here: 40.8 us
  Pallas kernels  38.9 us (95%)
  local copies, waits for them, and re-layouts  1.22 us (3%)
  between operations  0.64 us (2%)
    pallas_call x1, Pallas kernels, body(): pl.pallas_call(kernel, out_shape=(jax.ShapeDtypeStruct((OWN, width), F32)...  38.9 us
    unnamed x2, local copies, waits for them, and re-layouts  1.22 us

profile of v3, /device:TPU:1, one launch (start us, length us, event | category | flops | bytes accessed | tf_op | source)
XLA Modules:
  0.0 40.8 jit_solution(2010224401625193323)
XLA Ops:
  0.6 38.9 %shard_map.77 = (f32[16,768]{1,0:T(8,128)S(1)}, f32[16,96]{1,0:T(8,128)S(1)}) custom-call(bf16[1024,768]{1,0:T(8,128)(2,1)} %vec_hbm.1, bf16[4,8,2,16,768]{4,3,2,1,0:T(8,128)(2,1)} %bitcast.8, bf16[768,768]{1,0:T(8,128)(2,1)} %rot_hbm.1, f32[8,128]{1,0:T(8,128)} %bitcast.10, s32[8,128]{1,0:T(8,128)} %bitcast.11, s32[8,8,128]{2,1,0:T(8,128)} %bitcast.9), custom_call_target="tpu_custom_call" | custom-call | tf_op jit(solution)/shard_map/pallas_call | solution.py:396
  39.6 0.6 %copy.10 = f32[1,16,768]{2,1,0:T(8,128)} copy(f32[1,16,768]{2,1,0:T(8,128)S(1)} %bitcast.6) | data formatting | bytes 98304
  40.2 0.6 %copy.11 = f32[1,16,96]{2,1,0:T(8,128)} copy(f32[1,16,96]{2,1,0:T(8,128)S(1)} %bitcast.7) | data formatting | bytes 12288

commit v4 on v3

--- a/solution.py
+++ b/solution.py
@@ -39,7 +39,7 @@
     vec, cent, rot, prior, assign, owner, score, prob, weight, moment,
     stat_out, stat_in, rows_out, rows_in, turned_rows,
     own, own_m, snd, snd_m, rcv, rcv_m,
-    xs0, xs1, xr0, xr1, zs0, zs1, zs2, zr0, zr1, zr2, last, last_in,
+    xs0, xs1, xr0, xr1, zs0, zs1, zs2, zr0, zr1, zr2, last, last_in, kept,
     load_sem, send_sem, recv_sem,
 ):
     xs, xr, zs, zr = (xs0, xs1), (xr0, xr1), (zs0, zs1, zs2), (zr0, zr1, zr2)
@@ -193,8 +193,9 @@
         return remote(xs[q].at[j], xr[q].at[j], 4 + q, 7 + 2 * q + (j > 1), x_side[j % 2])
 
     def z_copy(q, j):
-        return remote(zs[q].at[j - 1], zr[q].at[j - 1], 6 + q, 11 + q,
-                      {"dp_1": lax.rem(pz + j, NZ)})
+        relayed = q != 1 and j == 4
+        return remote(zs[q].at[j - 1], zr[q].at[j - 1], 6 + q, 15 + q // 2 if relayed else 11 + q,
+                      {"dp_1": lax.rem(pz + (6 if relayed else j), NZ)})
 
     def last_copy(j):
         return remote(last.at[j], last_in.at[j - 1], 9, 14, {"dp_0": lax.rem(px + j, NX)})
@@ -221,7 +222,7 @@
         high = mass.astype(BF16).astype(F32)
         return jnp.where(lane == span, high, jnp.where(lane == span + 1, mass - high, a))
 
-    def moments():
+    def owners():
         wait_all(rows_in, recv_sem.at[1])
         got = jnp.concatenate([rows_out[py]] + [rows_in[j] for j in range(NY - 1)], axis=1)
         turned_rows[...] = got[0:span].astype(F32)
@@ -229,10 +230,12 @@
         q = iota((64, 1), 0)
         qc, qx, qz = q // 32, (q // 8) % 4, q % 8
         wanted = (((px + qx) % NX) * NZ + (pz + qz) % NZ) * NC + (pc + qc) % NC
-        chosen = as_bf16(wanted.astype(F32) == holders)
+        return as_bf16(wanted.astype(F32) == holders)
+
+    def moments(chosen, pairs):
         filler = jnp.zeros((128 - span, rows), BF16)
         by_owner = moment.reshape(64, OWN, 128)
-        for pair in range(SUB // 2):
+        for pair in pairs:
             pieces = []
             for a in (2 * pair, 2 * pair + 1):
                 for m in range(span // SUB):
@@ -243,6 +246,8 @@
             both = dot(chosen, jnp.concatenate(pieces, axis=0), ((1,), (1,)))
             for side in range(2):
                 by_owner[:, 2 * pair + side, :] = both[:, 128 * side : 128 * (side + 1)]
+
+    def moments_core():
         mass = jnp.sum(weight[...], axis=1, keepdims=True)
         both = split_mass(moment[...] + jnp.where(iota((rows, 128), 1) == span, mass, 0.0))
         snd_m[...] = both[512:].astype(BF16)
@@ -288,29 +293,45 @@
         high = own[64:128, columns(q)] + xr[q][2].astype(F32) + xr[q][5].astype(F32)
         block = [part[16 * j : 16 * (j + 1)] for part in (low, high) for j in range(4)]
         for j in (4, 3, 5, 2, 6, 1, 7):
+            if q == 0 and j == 6:
+                own[96:112, columns(q)] = block[j]
+                continue
             zs[q][j - 1] = block[j].astype(BF16)
             z_copy(q, j).start()
         own[0:OWN, columns(q)] = block[0]
 
+    def z_relay():
+        wait_all(zr[0].at[pl.ds(3, 1)], recv_sem.at[15])
+        zs[0][5] = (own[96:112, columns(0)] + zr[0][3].astype(F32)).astype(BF16)
+        z_copy(0, 6).start()
+
     def finish(q):
-        wait_all(zr[q], recv_sem.at[11 + q])
+        wait_all(zr[q] if q else zr[q].at[pl.ds(0, 6)], recv_sem.at[11 + q])
         got = own[0:OWN, columns(q)]
         for j in range(NZ - 1):
-            got = got + zr[q][j].astype(F32)
+            if q or j != 3:
+                got = got + zr[q][j].astype(F32)
         return got
 
     def moments_z():
         moment_copy.wait_recv()
         got = split_mass(own_m[...] + rcv_m[...].astype(F32)).reshape(NX, NZ, OWN, 128)
-        for j in (4, 3, 5, 2, 6, 1, 7):
+        for j in (4, 3, 5, 2, 1, 7):
             zs[2][j - 1] = got[:, j].astype(BF16)
             z_copy(2, j).start()
         last[...] = got[:, 0]
+        kept[...] = got[:, 6]
+
+    def moments_relay():
+        wait_all(zr[2].at[pl.ds(3, 1)], recv_sem.at[16])
+        got = (kept[...] + zr[2][3].astype(F32)).reshape(NX * OWN, 128)
+        zs[2][5] = split_mass(got).reshape(NX, OWN, 128).astype(BF16)
+        z_copy(2, 6).start()
 
     def moments_x():
         got = last[...]
-        wait_all(zr[2], recv_sem.at[13])
-        for j in range(NZ - 1):
+        wait_all(zr[2].at[pl.ds(0, 6)], recv_sem.at[13])
+        for j in (0, 1, 2, 4, 5, 6):
             got = got + zr[2][j].astype(F32)
         last[...] = got
         for j in (2, 1, 3):
@@ -333,14 +354,21 @@
     staged(sums, 3)
     staged(x_plain, 0)
     staged(sums, 0)
+    with scope("moments_1"):
+        chosen = owners()
+        moments(chosen, range(0, 4))
     staged(x_plain, 1)
-    staged(near)
-    staged(moments)
+    with scope("moments_2"):
+        moments(chosen, range(4, 8))
+        moments_core()
     staged(x_add, 0)
     staged(x_add, 1)
+    staged(near)
     staged(moments_z)
     staged(z_send, 0)
+    staged(moments_relay)
     staged(z_send, 1)
+    staged(z_relay)
     staged(moments_x)
     parts = [staged(finish, 0), staged(finish, 1), staged(moments_end)]
     lane = iota((OWN, 128), 1)
@@ -392,7 +420,8 @@
     turns = [pltpu.VMEM((NZ - 1, OWN, 384), BF16)] * 2
     turns += [pltpu.VMEM((NZ - 1, NX, OWN, 128), BF16)]
     scratch += turns * 2 + [pltpu.VMEM((NX, OWN, 128), F32), pltpu.VMEM((NX - 1, OWN, 128), F32)]
-    scratch += [dma((9,)), dma((14,)), dma((15,))]
+    scratch += [pltpu.VMEM((NX, OWN, 128), F32)]
+    scratch += [dma((9,)), dma((14,)), dma((17,))]
     updated, moments = pl.pallas_call(
         kernel,
         out_shape=(

time: 40.9 us -> 40.1 us (0.980)
  Pallas kernels: 38.9 us -> 37.7 us
    pallas_call x1, Pallas kernels: 38.9 us -> 37.7 us  [body(): pl.pallas_call(kernel, out_shape=(jax.ShapeDtypeStruct((OWN, width), F32)...]
where the time goes in v4:
time: 40.1 us; the launch traced here: 39.6 us
  Pallas kernels  37.7 us (94%)
  local copies, waits for them, and re-layouts  1.22 us (3%)
  between operations  0.64 us (2%)
    pallas_call x1, Pallas kernels, body(): pl.pallas_call(kernel, out_shape=(jax.ShapeDtypeStruct((OWN, width), F32)...  37.7 us
    unnamed x2, local copies, waits for them, and re-layouts  1.22 us

profile of v4, /device:TPU:1, one launch (start us, length us, event | category | flops | bytes accessed | tf_op | source)
XLA Modules:
  0.0 39.6 jit_solution(7077974411073247184)
XLA Ops:
  0.6 37.7 %shard_map.77 = (f32[16,768]{1,0:T(8,128)S(1)}, f32[16,96]{1,0:T(8,128)S(1)}) custom-call(bf16[1024,768]{1,0:T(8,128)(2,1)} %vec_hbm.1, bf16[4,8,2,16,768]{4,3,2,1,0:T(8,128)(2,1)} %bitcast.8, bf16[768,768]{1,0:T(8,128)(2,1)} %rot_hbm.1, f32[8,128]{1,0:T(8,128)} %bitcast.10, s32[8,128]{1,0:T(8,128)} %bitcast.11, s32[8,8,128]{2,1,0:T(8,128)} %bitcast.9), custom_call_target="tpu_custom_call" | custom-call | tf_op jit(solution)/shard_map/pallas_call | solution.py:425
  38.4 0.6 %copy.10 = f32[1,16,768]{2,1,0:T(8,128)} copy(f32[1,16,768]{2,1,0:T(8,128)S(1)} %bitcast.6) | data formatting | bytes 98304
  39.0 0.6 %copy.11 = f32[1,16,96]{2,1,0:T(8,128)} copy(f32[1,16,96]{2,1,0:T(8,128)S(1)} %bitcast.7) | data formatting | bytes 12288

commit v5 on v4

--- a/solution.py
+++ b/solution.py
@@ -14,6 +14,7 @@
 DP = ("dp_0", "dp_1", "dp_2")
 NX, NZ, NC, NY = 4, 8, 2, 8
 OWN = 16
+EDGES = (0, 256, 768)
 SUB = 16
 scope = contextlib.nullcontext
 
@@ -260,7 +261,7 @@
         return own[at, :] + rcv[at, :].astype(F32)
 
     def columns(q):
-        return slice(384 * q, 384 * (q + 1))
+        return slice(EDGES[q], EDGES[q + 1])
 
     def x_far():
         got = joined(2).astype(BF16)
@@ -416,8 +417,9 @@
         pltpu.VMEM((span, rows), F32),
     ]
     scratch += [pltpu.VMEM((half, w), kind) for kind in (F32, BF16, BF16) for w in (width, 128)]
-    scratch += [pltpu.VMEM((6, 64, 384), BF16)] * 4
-    turns = [pltpu.VMEM((NZ - 1, OWN, 384), BF16)] * 2
+    widths = [b - a for a, b in zip(EDGES, EDGES[1:])]
+    scratch += [pltpu.VMEM((6, 64, w), BF16) for w in widths] * 2
+    turns = [pltpu.VMEM((NZ - 1, OWN, w), BF16) for w in widths]
     turns += [pltpu.VMEM((NZ - 1, NX, OWN, 128), BF16)]
     scratch += turns * 2 + [pltpu.VMEM((NX, OWN, 128), F32), pltpu.VMEM((NX - 1, OWN, 128), F32)]
     scratch += [pltpu.VMEM((NX, OWN, 128), F32)]

time: 40.1 us -> 40 us (level)
  no operation moved by 1% of the time
where the time goes in v5:
time: 40 us; the launch traced here: 39.8 us
  Pallas kernels  38 us (95%)
  local copies, waits for them, and re-layouts  1.22 us (3%)
  between operations  0.64 us (2%)
    pallas_call x1, Pallas kernels, body(): pl.pallas_call(kernel, out_shape=(jax.ShapeDtypeStruct((OWN, width), F32)...  38 us
    unnamed x2, local copies, waits for them, and re-layouts  1.22 us

profile of v5, /device:TPU:1, one launch (start us, length us, event | category | flops | bytes accessed | tf_op | source)
XLA Modules:
  0.0 39.8 jit_solution(13581527962500383735)
XLA Ops:
  0.6 38.0 %shard_map.77 = (f32[16,768]{1,0:T(8,128)S(1)}, f32[16,96]{1,0:T(8,128)S(1)}) custom-call(bf16[1024,768]{1,0:T(8,128)(2,1)} %vec_hbm.1, bf16[4,8,2,16,768]{4,3,2,1,0:T(8,128)(2,1)} %bitcast.8, bf16[768,768]{1,0:T(8,128)(2,1)} %rot_hbm.1, f32[8,128]{1,0:T(8,128)} %bitcast.10, s32[8,128]{1,0:T(8,128)} %bitcast.11, s32[8,8,128]{2,1,0:T(8,128)} %bitcast.9), custom_call_target="tpu_custom_call" | custom-call | tf_op jit(solution)/shard_map/pallas_call | solution.py:427
  38.6 0.6 %copy.10 = f32[1,16,768]{2,1,0:T(8,128)} copy(f32[1,16,768]{2,1,0:T(8,128)S(1)} %bitcast.6) | data formatting | bytes 98304
  39.2 0.6 %copy.11 = f32[1,16,96]{2,1,0:T(8,128)} copy(f32[1,16,96]{2,1,0:T(8,128)S(1)} %bitcast.7) | data formatting | bytes 12288
